TPU v7x, 128 devices: a whole 4x4x4 slice. The times are simulated.
128 devices in a mesh: row: 16 (over y, x), col: 8 (over z, core).
Axes of the slice: x: 4, y: 4, z: 4, core: 2. Of those that a mesh axis runs over, the one named last changes fastest.
Arguments:
- panel_cols: float32 [256, 16384], P('col', 'row'), as said below
- window_cols: float32 [16384, 16384], P('col', 'row'), may hold values from -6 to 6
Outputs:
- triangle: float32 [256, 256], replicated
- top_rows: float32 [16384, 256], P(('col', 'row'))
- residual: float32 [16384, 16384], P('col', 'row')
Inputs may be any that keep to these rules, and one draw needn't show every extreme that they name: `panel_cols`: the 256 rows are linearly independent over the 1024 columns of every block of row.
All inputs are finite; a program needn't handle non-finite values.
Results may differ from a plain program's by a relative error of at most 0.000084.
Values sent between devices are 32-bit elements; how exact they have to be, the bound alone decides.
A program may use at most 64 MiB of HBM per device.

v0:
```python
import jax
import jax.numpy as jnp
from jax import lax
from jax.sharding import PartitionSpec as P

precise = lax.Precision.HIGHEST


def outer_sum(left, right):
    return lax.dot_general(
        left, right, (((1,), (1,)), ((), ())), precision=precise, preferred_element_type=jnp.float32
    )


def lower_inverse(lower_part):
    identity = jnp.eye(lower_part.shape[0], dtype=jnp.float32)
    return lax.linalg.triangular_solve(lower_part, identity, left_side=True, lower=True)


def local(panel_cols, window_cols):
    slab = window_cols.shape[0]
    whole = lax.all_gather(panel_cols, "col", axis=0, tiled=True)
    cross = outer_sum(window_cols, whole)
    gram_local = outer_sum(whole, whole)
    gram_total, cross_total = lax.psum((gram_local, cross), "row")
    lower_part = jnp.linalg.cholesky(gram_total)
    inverse = lower_inverse(lower_part)
    top_all = outer_sum(cross_total, inverse)
    share_rows = slab // lax.axis_size("row")
    top_rows = lax.dynamic_slice_in_dim(top_all, lax.axis_index("row") * share_rows, share_rows, 0)
    combined = jnp.dot(top_all, inverse, precision=precise, preferred_element_type=jnp.float32)
    residual = window_cols - jnp.dot(
        combined, whole, precision=precise, preferred_element_type=jnp.float32
    )
    return (lower_part.T, top_rows, residual)


def solution(mesh):
    return jax.shard_map(
        local,
        mesh=mesh,
        in_specs=(P("col", "row"), P("col", "row")),
        out_specs=(P(), P(("col", "row"), None), P("col", "row")),
        check_vma=False,
    )
```

profile of v0, /device:TPU:0, one launch (start us, length us, event | category | flops | bytes accessed | tf_op | source)
XLA Modules:
  0.0 238.2 jit_solution(10998402472128093950)
XLA Ops:
  7.2 0.0 all-gather.2.cloned.1.call-start
  7.2 0.7 all-gather.2.cloned.1.call-update
  7.9 0.0 all-reduce.4.cloned.1.call-start
  7.9 27.7 %all-gather.2.cloned.1.call-done = f32[256,1024]{1,0:T(8,128)} async-done(((f32[32,1024]{1,0:T(8,128)}), f32[256,1024]{1,0:T(8,128)}) %all-gather.2.cloned.1.call-update) | async-done | bytes 1048592 | tf_op jit(solution)/shard_map/all_gather | solution.py:22
  35.7 0.0 copy-start
  35.7 3.4 %fusion.15 = f32[256,256]{0,1:T(8,128)} fusion(f32[256,1024]{1,0:T(8,128)} %all-gather.2.cloned.1.call-done), kind=kOutput, calls=%fused_computation.38 | convolution fusion | flops 805306368 | bytes 1310720 | tf_op jit(solution)/shard_map/dot_general | solution.py:10
  39.0 0.0 copy-done
  39.0 10.1 %fusion.16 = f32[2048,256]{1,0:T(8,128)} fusion(f32[2048,1024]{1,0:T(8,128)} %param.3, f32[256,1024]{1,0:T(8,128)S(1)} %copy-done), kind=kOutput, calls=%fused_computation.39 | convolution fusion | flops 6442450944 | bytes 11534336 | tf_op jit(solution)/shard_map/dot_general | solution.py:10
  49.1 0.0 all-reduce.4.cloned.1.call-update
  49.2 91.9 %all-reduce.4.cloned.1.call-done = (f32[256,256]{0,1:T(8,128)}, f32[2048,256]{1,0:T(8,128)}) async-done(((f32[256,256]{0,1:T(8,128)}, f32[2048,256]{1,0:T(8,128)}), (f32[256,256]{0,1:T(8,128)}, f32[2048,256]{1,0:T(8,128)})) %all-reduce.4.cloned.1.call-update) | async-done | bytes 2359312 | tf_op jit(solution)/shard_map/psum | solution.py:25
  141.1 1.1 copy.6
  142.2 1.0 fusion
  143.2 0.0 copy-start.3
  143.2 0.7 copy-done.3
  143.9 11.7 %cholesky.50 = f32[128,128]{1,0:T(8,128)S(1)} custom-call(f32[128,128]{1,0:T(8,128)S(1)} %cholesky.118), custom_call_target="Cholesky" | custom-call | tf_op jit(solution)/shard_map/jit(cholesky)/cholesky | solution.py:26
  155.6 0.0 copy-start.1
  155.7 10.4 %custom-call.14 = f32[1,128,128]{1,2,0:T(8,128)} custom-call(f32[1,128,128]{2,1,0:T(8,128)S(1)} %get-tuple-element.31), custom_call_target="InvertDiagBlocksLowerTriangular" | custom-call | tf_op jit(solution)/shard_map/jit(cholesky)/cholesky | solution.py:26
  166.2 1.1 constant_dynamic-update-slice_fusion
  167.2 1.7 convolution_subtract_fusion.2
  169.0 12.5 %cholesky.105 = f32[128,128]{1,0:T(8,128)S(1)} custom-call(f32[128,128]{1,0:T(8,128)} %convolution_subtract_fusion.2), custom_call_target="Cholesky" | custom-call | tf_op jit(solution)/shard_map/jit(cholesky)/cholesky | solution.py:26
  181.6 0.0 copy-start.2
  181.6 0.6 compare_reduce_fusion
  183.5 0.0 copy-done.2
  183.5 1.7 fusion.1
  185.2 1.8 copy.7
  187.0 0.1 triangular_solve.44
  187.1 5.2 %while.1 = (s32[]{:T(128)}, f32[256,256]{1,0:T(8,128)S(1)}, s32[2,2]{1,0:T(2,128)S(1)}, f32[2,128,128]{2,1,0:T(8,128)}, s32[]{:T(128)}) while((s32[]{:T(128)}, f32[256,256]{1,0:T(8,128)S(1)}, s32[2,2]{1,0:T(2,128)S(1)}, f32[2,128,128]{2,1,0:T(8,128)}, s32[]{:T(128)}) %tuple.29), condition=%wide.while_cond, body=%wide.while_body.sunk | while | flops 2 | bytes 132205 | solution.py:17
  187.1 0.6 fusion.30
  187.7 2.0 bitcast_dynamic-update-slice_fusion.2
  189.7 0.6 fusion.30
  190.2 2.0 bitcast_dynamic-update-slice_fusion.2
  192.2 21.1 %custom-call.15 = f32[2,128,128]{1,2,0:T(8,128)} custom-call(f32[2,128,128]{2,1,0:T(8,128)} %get-tuple-element.10), custom_call_target="InvertDiagBlocksLowerTriangular" | custom-call | tf_op jit(solution)/shard_map/triangular_solve | solution.py:17
  213.3 1.1 fusion.5
  214.5 0.3 convolution_subtract_fusion.1
  214.7 1.2 fusion.8
  215.9 0.0 copy-done.1
  215.9 1.9 fusion.4
  217.8 1.9 fusion.3
  219.7 0.7 constant_dynamic-slice_fusion.1
  220.4 11.0 %convolution_subtract_fusion = f32[2048,1024]{1,0:T(8,128)} fusion(f32[2048,1024]{1,0:T(8,128)} %param.3, f32[2048,256]{1,0:T(8,128)S(1)} %fusion.3, f32[256,1024]{1,0:T(8,128)S(1)} %copy-done), kind=kOutput, calls=%fused_computation.2 | convolution fusion | flops 6444548096 | bytes 19922944 | tf_op jit(solution)/shard_map/dot_general | solution.py:32
  (9 shorter events, 0.1 us)
Async XLA Ops:
  7.2 28.5 %all-gather.2.cloned.1.call-start = ((), (), s32[]{:S(2)}) async-start(), calls=%async_computation | async-start | bytes 1179648 | tf_op jit(solution)/shard_map/all_gather | solution.py:22
  7.9 133.2 %all-reduce.4.cloned.1.call-start = ((), (), s32[]{:S(2)}) async-start(), calls=%async_computation.1 | async-start | bytes 4718592 | tf_op jit(solution)/shard_map/psum | solution.py:25
  35.7 3.4 %copy-start = (f32[256,1024]{1,0:T(8,128)S(1)}, f32[256,1024]{1,0:T(8,128)}, u32[]{:S(2)}) copy-start(f32[256,1024]{1,0:T(8,128)} %all-gather.2.cloned.1.call-done) | copy-start | bytes 3145732
  143.2 0.7 copy-start.3
  155.6 60.2 %copy-start.1 = (f32[2048,256]{1,0:T(8,128)S(1)}, f32[2048,256]{1,0:T(8,128)}, u32[]{:S(2)}) copy-start(f32[2048,256]{1,0:T(8,128)} %get-tuple-element.23) | copy-start | bytes 6291460
  181.6 1.9 copy-start.2
Sparse Core Ops, SparseCore 0:
  9.7 25.9 all-gather.1
  49.3 91.8 all-reduce.3
where the time goes:
time: 239 us; the launch traced here: 238 us
  waiting for transfers between devices  120 us (50%)
  other arithmetic  59.2 us (25%)
  matrix products  33.6 us (14%)
  between operations  15.5 us (6%)
  local copies, waits for them, and re-layouts  9.51 us (4%)
    psum x1, waiting for transfers between devices, local(): gram_total, cross_total = lax.psum((gram_local, cross), 'row')  91.9 us
    another operation x6, other arithmetic, local(): lower_part = jnp.linalg.cholesky(gram_total)  35.4 us
    all_gather x1, waiting for transfers between devices, local(): whole = lax.all_gather(panel_cols, 'col', axis=0, tiled=True)  27.7 us
    another operation x3, other arithmetic, lower_inverse(): lax.linalg.triangular_solve(lower_part, identity, left_side=True, lower=T...  22.8 us
    dot_general x3, matrix products, outer_sum(): lax.dot_general(left, right, (((1,), (1,)), ((), ())), precision=precise,...  15.4 us
    dot_general x1, matrix products, local(): jnp.dot(combined, whole, precision=precise, preferred_element_type=jnp.fl...  11 us
    another operation x6, local copies, waits for them, and re-layouts  5.17 us
  transfers between devices with their start and end apart: 2, of which 2 were waited for; matrix products, arithmetic and copies ran while one was open for 0% of the time, Pallas kernels for 0%

commit v1 on v0

v1 whole, which is shorter than its diff:
```python
import jax
import jax.numpy as jnp
from jax import lax
from jax.experimental import pallas as pl
from jax.experimental.pallas import tpu as pltpu
from jax.sharding import PartitionSpec as P

MESH = pl.DeviceIdType.MESH
HIGHEST = lax.Precision.HIGHEST
F32 = jnp.float32
BF16 = jnp.bfloat16

N = 256
SLAB = 2048
DEPTH = 1024
PIECE = 32
CHUNKS = 2
S1 = 256 // CHUNKS
S2 = S1 // 4
BLOCK = 32


def dot_nt(a, b, precision=None):
    return lax.dot_general(a, b, (((1,), (1,)), ((), ())), precision=precision, preferred_element_type=F32)


def dot_nn(a, b, precision=None):
    return lax.dot_general(a, b, (((1,), (0,)), ((), ())), precision=precision, preferred_element_type=F32)


def dot_tn(a, b, precision=None):
    return lax.dot_general(a, b, (((0,), (0,)), ((), ())), precision=precision, preferred_element_type=F32)


def split(v):
    high = v.astype(BF16)
    return high, (v - high.astype(F32)).astype(BF16)


N_PANEL = 13
N_GRAM = 13
N_CROSS = 2 * CHUNKS * 24


def body(
    panel_ref, w_hbm,
    u_out, top_out, ch_out, cl_out, bh_out, bl_out,
    w_ref, wh_ref, wl_ref, a_ref, ah_ref, al_ref, gx_ref, gy_ref, gz_ref, t_ref,
    c_ref, f_ref, r1_ref, r2_ref, w_sem, send_sem, recv_sem,
):
    row = lax.axis_index("row")
    col = lax.axis_index("col")
    y, x = lax.div(row, 4), lax.rem(row, 4)
    z, k = lax.div(col, 2), lax.rem(col, 2)

    def step(v, d):
        return lax.rem(v + d, 4)

    def at_x(d):
        return (y * 4 + step(x, d), col)

    def at_y(d):
        return (step(y, d) * 4 + x, col)

    def piece(d, core):
        return step(z, d) * 2 + core

    partner = (row, z * 2 + 1 - k)
    up, down = (row, piece(1, k)), (row, piece(3, k))

    for b in range(8):
        pltpu.make_async_copy(w_hbm.at[pl.ds(b * 256, 256), :], w_ref.at[pl.ds(b * 256, 256), :], w_sem.at[b]).start()

    barrier = pltpu.get_barrier_semaphore()
    others = [at_x(d) for d in (1, 2, 3)] + [at_y(d) for d in (1, 2, 3)]
    others += [(row, lax.rem(col + d, 8)) for d in range(1, 8)]
    for dev in others:
        pl.semaphore_signal(barrier, inc=1, device_id=dev, device_id_type=MESH)
    pl.semaphore_wait(barrier, len(others))

    sent = []

    def send(index, src, dst, dev):
        copy = pltpu.make_async_remote_copy(
            src_ref=src, dst_ref=dst, send_sem=send_sem.at[index], recv_sem=recv_sem.at[index],
            device_id=dev, device_id_type=MESH,
        )
        copy.start()
        sent.append(copy)
        return copy

    half = (pl.ds(0, 16), pl.ds(16, 16))
    own = {}
    own["up0"] = send(0, panel_ref.at[half[0]], a_ref.at[col, half[0]], up)
    own["down1"] = send(1, panel_ref.at[half[1]], a_ref.at[col, half[1]], down)
    own["up1"] = send(2, panel_ref.at[half[1]], a_ref.at[col, half[1]], up)
    own["down0"] = send(3, panel_ref.at[half[0]], a_ref.at[col, half[0]], down)
    own["partner"] = send(4, panel_ref, a_ref.at[col], partner)
    a_ref[col] = panel_ref[...]

    for b in range(8):
        rows = pl.ds(b * 256, 256)
        pltpu.make_async_copy(w_hbm.at[rows, :], w_ref.at[rows, :], w_sem.at[b]).wait()
        high, low = split(w_ref[rows, :])
        wh_ref[rows, :] = high
        wl_ref[rows, :] = low

    below, above, far = piece(3, k), piece(1, k), piece(2, k)

    def pass_on(index, who, h, dev):
        return send(index, a_ref.at[who, half[h]], a_ref.at[who, half[h]], dev)

    own["up0"].wait_recv()
    relay0 = pass_on(5, below, 0, up)
    own["down1"].wait_recv()
    relay1 = pass_on(6, above, 1, down)
    forwards = [pass_on(7, below, 0, partner), pass_on(8, above, 1, partner)]
    own["up1"].wait_recv()
    forwards.append(pass_on(9, below, 1, partner))
    own["down0"].wait_recv()
    forwards.append(pass_on(10, above, 0, partner))
    relay0.wait_recv()
    forwards.append(pass_on(11, far, 0, partner))
    relay1.wait_recv()
    forwards.append(pass_on(12, far, 1, partner))
    own["partner"].wait_recv()
    for copy in forwards:
        copy.wait_recv()

    panel = a_ref[...].reshape(N, DEPTH)
    high, low = split(panel)
    ah_ref[...] = high
    al_ref[...] = low

    base = N_PANEL
    gx_ref[x] = dot_nt(panel_ref[...], panel, HIGHEST)
    gram_x = [send(base + d - 1, gx_ref.at[x], gx_ref.at[x], at_x(d)) for d in (1, 2, 3)]

    def gram_to_y():
        for copy in gram_x:
            copy.wait_recv()
        gy_ref[y] = (gx_ref[0] + gx_ref[1]) + (gx_ref[2] + gx_ref[3])
        return [send(base + 3 + d - 1, gy_ref.at[y], gy_ref.at[y], at_y(d)) for d in (1, 2, 3)]

    def gram_to_col(gram_y):
        for copy in gram_y:
            copy.wait_recv()
        gz_ref[col] = (gy_ref[0] + gy_ref[1]) + (gy_ref[2] + gy_ref[3])
        return [send(base + 6 + d - 1, gz_ref.at[col], gz_ref.at[col], (row, lax.rem(col + d, 8))) for d in range(1, 8)]

    def gram_done(gram_z):
        for copy in gram_z:
            copy.wait_recv()
        t_ref[:, :N] = gz_ref[...].reshape(N, N)
        rows_at = lax.broadcasted_iota(jnp.int32, (N, N), 0)
        cols_at = lax.broadcasted_iota(jnp.int32, (N, N), 1)
        t_ref[:, N:] = jnp.where(rows_at == cols_at, 1.0, 0.0).astype(F32)

    def factor(b):
        lo = b * BLOCK
        tile, shift = lo // 128 * 128, lo % 128
        e = t_ref[lo:lo + BLOCK, tile:tile + 128]
        if shift:
            e = pltpu.roll(e, 128 - shift, 1)
        sub = lax.broadcasted_iota(jnp.int32, (BLOCK, 128), 0)
        lane = lax.broadcasted_iota(jnp.int32, (BLOCK, 128), 1)
        e = jnp.where(lane < BLOCK, e, jnp.where(lane == sub + BLOCK, 1.0, 0.0).astype(F32))
        for j in range(BLOCK - 1):
            pivot_row = e[j:j + 1, :]
            pivot = jnp.broadcast_to(pivot_row[:, j:j + 1], (1, 128))
            column = jnp.broadcast_to(e[:, j:j + 1], (BLOCK, 128))
            e = e - jnp.where(sub > j, column, 0.0) * (pivot_row / pivot)
        diagonal = jnp.sum(jnp.where(lane == sub, e, 0.0), axis=1, keepdims=True)
        root = lax.rsqrt(diagonal)
        root = root * (1.5 - 0.5 * diagonal * root * root)
        e = e * root
        inverse = e[:, BLOCK:2 * BLOCK]
        done = dot_nn(inverse, t_ref[lo:lo + BLOCK, :], HIGHEST)
        t_ref[lo:lo + BLOCK, :] = done
        if lo + BLOCK < N:
            update = dot_tn(done[:, :N], done, HIGHEST)
            t_ref[lo + BLOCK:, :] -= update[lo + BLOCK:, :]

    def finish():
        rows_at = lax.broadcasted_iota(jnp.int32, (N, N), 0)
        cols_at = lax.broadcasted_iota(jnp.int32, (N, N), 1)
        u_out[...] = jnp.where(cols_at >= rows_at, t_ref[:, :N], 0.0)
        inverse = jnp.where(cols_at <= rows_at, t_ref[:, N:], 0.0)
        t_ref[:, N:] = inverse
        q = dot_nn(inverse, a_ref[...].reshape(N, DEPTH), HIGHEST)
        high, low = split(dot_tn(inverse, q, HIGHEST))
        bh_ref, bl_ref = bh_out, bl_out
        bh_ref[...] = high
        bl_ref[...] = low

    def rows_of(start, size, align):
        return pl.ds(pl.multiple_of(start, align), size)

    def product(part, d):
        where = rows_of(part * 1024 + step(y if part else x, d) * 256, 256, 256)
        wh, wl = wh_ref[where, :], wl_ref[where, :]
        ah, al = ah_ref[...], al_ref[...]
        c_ref[where, :] = (dot_nt(wh, al) + dot_nt(wl, ah)) + dot_nt(wh, ah)

    class Stream:
        def __init__(self, part, chunk):
            self.at = (at_y, at_x) if part else (at_x, at_y)
            self.me = (y, x) if part else (x, y)
            self.start = part * 1024 + chunk * S1
            self.index = N_PANEL + N_GRAM + (part * CHUNKS + chunk) * 24
            self.buf = (r1_ref.at[part, chunk], r2_ref.at[part, chunk])

        def place(self, axis, d, h, buf_rows=None):
            size = S2 if axis else S1
            start = self.start + self.me[0] * 256
            if axis:
                start = start + step(self.me[1], d) * S2
            else:
                start = self.start + step(self.me[0], d) * 256
            if h is None:
                return rows_of(start, size, size)
            return rows_of(start + h * (size // 2), size // 2, size // 2)

        def rs_send(self, axis, slot, src, d):
            return send(self.index + axis * 6 + slot, c_ref.at[src, :], self.buf[axis].at[slot], self.at[axis](d))

        def far_out(self, axis):
            self.rs = [None] * 6
            self.rs[0] = self.rs_send(axis, 0, self.place(axis, 2, 0), 1)
            self.rs[1] = self.rs_send(axis, 1, self.place(axis, 2, 1), 3)

        def near_out(self, axis):
            self.rs[2] = self.rs_send(axis, 2, self.place(axis, 1, 1), 1)
            self.rs[3] = self.rs_send(axis, 3, self.place(axis, 3, 0), 3)

        def relay(self, axis):
            for slot, (d, h) in enumerate(((1, 0), (3, 1))):
                self.rs[slot].wait_recv()
                where = self.place(axis, d, h)
                c_ref[where, :] += self.buf[axis][slot]
                self.rs[4 + slot] = self.rs_send(axis, 4 + slot, where, d)

        def gathered(self, axis, into):
            for slot in (2, 3, 4, 5):
                self.rs[slot].wait_recv()
            for h, (a, b) in enumerate(((3, 4), (2, 5))):
                where = self.place(axis, 0, h)
                into[where, :] = c_ref[where, :] + (self.buf[axis][a] + self.buf[axis][b])

        def ag_send(self, axis, slot, where, d):
            return send(self.index + 12 + axis * 6 + slot, f_ref.at[where, :], f_ref.at[where, :], self.at[axis](d))

        def spread(self, axis):
            self.ag = [
                self.ag_send(axis, 0, self.place(axis, 0, 0), 1),
                self.ag_send(axis, 1, self.place(axis, 0, 1), 3),
                self.ag_send(axis, 2, self.place(axis, 0, 1), 1),
                self.ag_send(axis, 3, self.place(axis, 0, 0), 3),
            ]

        def hand_on(self, axis):
            self.ag[0].wait_recv()
            self.ag.append(self.ag_send(axis, 4, self.place(axis, 3, 0), 1))
            self.ag[1].wait_recv()
            self.ag.append(self.ag_send(axis, 5, self.place(axis, 1, 1), 3))

        def spread_done(self, axis):
            for slot in (2, 3, 4, 5):
                self.ag[slot].wait_recv()

    streams = [[Stream(part, chunk) for part in range(2)] for chunk in range(CHUNKS)]

    def run(chunk, number):
        for s in streams[chunk]:
            if number == 0:
                s.far_out(0)
            elif number == 1:
                s.near_out(0)
            elif number == 2:
                s.relay(0)
            elif number == 3:
                s.gathered(0, c_ref)
                s.far_out(1)
                s.near_out(1)
            elif number == 4:
                s.relay(1)
            elif number == 5:
                s.gathered(1, f_ref)
                s.spread(1)
            elif number == 6:
                s.hand_on(1)
            elif number == 7:
                s.spread_done(1)
                s.spread(0)
            elif number == 8:
                s.hand_on(0)
            elif number == 9:
                s.spread_done(0)

    product(0, 2)
    product(1, 2)
    run(0, 0)
    gram_y = gram_to_y()
    run(1, 0)
    for d in (1, 3):
        product(0, d)
        product(1, d)
    run(0, 1)
    gram_z = gram_to_col(gram_y)
    run(1, 1)
    product(0, 0)
    product(1, 0)
    run(0, 2)
    gram_done(gram_z)
    factor(0)
    run(1, 2)
    for number in range(3, 9):
        run(0, number)
        factor(number - 2)
        run(1, number)
    factor(7)
    run(0, 9)
    finish()
    run(1, 9)

    for b in range(8):
        rows = pl.ds(b * 256, 256)
        high, low = split(f_ref[rows, :])
        ch_out[rows, :] = high
        cl_out[rows, :] = low
    top_out[...] = dot_nt(f_ref[rows_of(row * 128, 128, 128), :], t_ref[:, N:], HIGHEST)

    for copy in sent:
        copy.wait_send()


def gather_and_factor(panel_cols, window_cols):
    vmem = pl.BlockSpec(memory_space=pltpu.VMEM)
    count = N_PANEL + N_GRAM + N_CROSS
    return pl.pallas_call(
        body,
        out_shape=(
            jax.ShapeDtypeStruct((N, N), F32),
            jax.ShapeDtypeStruct((128, N), F32),
            jax.ShapeDtypeStruct((SLAB, N), BF16),
            jax.ShapeDtypeStruct((SLAB, N), BF16),
            jax.ShapeDtypeStruct((N, DEPTH), BF16),
            jax.ShapeDtypeStruct((N, DEPTH), BF16),
        ),
        in_specs=[vmem, pl.BlockSpec(memory_space=pl.ANY)],
        out_specs=(vmem,) * 6,
        scratch_shapes=[
            pltpu.VMEM((SLAB, DEPTH), F32),
            pltpu.VMEM((SLAB, DEPTH), BF16),
            pltpu.VMEM((SLAB, DEPTH), BF16),
            pltpu.VMEM((8, PIECE, DEPTH), F32),
            pltpu.VMEM((N, DEPTH), BF16),
            pltpu.VMEM((N, DEPTH), BF16),
            pltpu.VMEM((4, PIECE, N), F32),
            pltpu.VMEM((4, PIECE, N), F32),
            pltpu.VMEM((8, PIECE, N), F32),
            pltpu.VMEM((N, 2 * N), F32),
            pltpu.VMEM((SLAB, N), F32),
            pltpu.VMEM((SLAB, N), F32),
            pltpu.VMEM((2, CHUNKS, 6, S1 // 2, N), F32),
            pltpu.VMEM((2, CHUNKS, 6, S2 // 2, N), F32),
            pltpu.SemaphoreType.DMA((8,)),
            pltpu.SemaphoreType.DMA((count,)),
            pltpu.SemaphoreType.DMA((count,)),
        ],
        compiler_params=pltpu.CompilerParams(
            collective_id=0, has_side_effects=True, vmem_limit_bytes=56 * 2**20
        ),
        name="gather_and_factor",
    )(panel_cols, window_cols)


def residual_body(w_ref, ch_ref, cl_ref, bh_ref, bl_ref, out_ref):
    ch, cl, bh, bl = ch_ref[...], cl_ref[...], bh_ref[...], bl_ref[...]
    out_ref[...] = w_ref[...] - ((dot_nn(ch, bl) + dot_nn(cl, bh)) + dot_nn(ch, bh))


def subtract(window_cols, ch, cl, bh, bl):
    rows = 256
    return pl.pallas_call(
        residual_body,
        out_shape=jax.ShapeDtypeStruct((SLAB, DEPTH), F32),
        grid=(SLAB // rows,),
        in_specs=[
            pl.BlockSpec((rows, DEPTH), lambda i: (i, 0)),
            pl.BlockSpec((rows, N), lambda i: (i, 0)),
            pl.BlockSpec((rows, N), lambda i: (i, 0)),
            pl.BlockSpec((N, DEPTH), lambda i: (0, 0)),
            pl.BlockSpec((N, DEPTH), lambda i: (0, 0)),
        ],
        out_specs=pl.BlockSpec((rows, DEPTH), lambda i: (i, 0)),
        name="subtract",
    )(window_cols, ch, cl, bh, bl)


def local(panel_cols, window_cols):
    triangle, top_rows, ch, cl, bh, bl = gather_and_factor(panel_cols, window_cols)
    residual = subtract(window_cols, ch, cl, bh, bl)
    return triangle, top_rows, residual


def solution(mesh):
    return jax.shard_map(
        local,
        mesh=mesh,
        in_specs=(P("col", "row"), P("col", "row")),
        out_specs=(P(), P(("col", "row"), None), P("col", "row")),
        check_vma=False,
    )
```

time: 239 us -> 95.8 us (0.40)
  waiting for transfers between devices: 120 us -> 0 us
  Pallas kernels: 0 us -> 92.8 us
  other arithmetic: 59.2 us -> 0 us
  matrix products: 33.6 us -> 0 us
  between operations: 15.5 us -> 0.66 us
  local copies, waits for them, and re-layouts: 9.51 us -> 1.37 us
    pallas_call x0 -> x2, Pallas kernels: none -> 92.8 us  [the longest x1 80.9 us: gather_and_factor(): pl.pallas_call(body, out_shape=(jax.ShapeDtypeStruct((N, N), F32), jax.Sh...]
    psum x1 -> x0, waiting for transfers between devices: 91.9 us -> none  [local(): gram_total, cross_total = lax.psum((gram_local, cross), 'row')]
    another operation x9 -> x0, other arithmetic: 58.2 us -> none  [the longest x6 35.4 us: local(): lower_part = jnp.linalg.cholesky(gram_total)]
    dot_general x5 -> x0, matrix products: 28.2 us -> none  [the longest x3 15.4 us: outer_sum(): lax.dot_general(left, right, (((1,), (1,)), ((), ())), precision=precise,...]
    all_gather x1 -> x0, waiting for transfers between devices: 27.7 us -> none  [local(): whole = lax.all_gather(panel_cols, 'col', axis=0, tiled=True)]
    another operation x5 -> x0, matrix products: 5.34 us -> none  [the longest x2 2.82 us: local(): lower_part = jnp.linalg.cholesky(gram_total)]
    another operation x9 -> x0, local copies, waits for them, and re-layouts: 5.27 us -> none
  transfers between devices with their start and end apart: 2 -> 0, of which waited for: 2 -> 0; matrix products, arithmetic and copies ran while one was open for 0% -> 0% of each run, Pallas kernels for 0% -> 0%
where the time goes in v1:
time: 95.8 us; the launch traced here: 94.8 us
  Pallas kernels  92.8 us (97%)
  local copies, waits for them, and re-layouts  1.37 us (1%)
    pallas_call x1, Pallas kernels, gather_and_factor(): pl.pallas_call(body, out_shape=(jax.ShapeDtypeStruct((N, N), F32), jax.Sh...  80.9 us
    pallas_call x1, Pallas kernels, subtract(): pl.pallas_call(residual_body, out_shape=jax.ShapeDtypeStruct((SLAB, DEPTH...  11.9 us

profile of v1, /device:TPU:0, one launch (start us, length us, event | category | flops | bytes accessed | tf_op | source)
XLA Modules:
  0.0 94.8 jit_solution(7118628698313084806)
XLA Ops:
  0.6 80.9 %gather_and_factor.1 = (f32[256,256]{1,0:T(8,128)}, f32[128,256]{1,0:T(8,128)}, bf16[2048,256]{1,0:T(8,128)(2,1)}, bf16[2048,256]{1,0:T(8,128)(2,1)}, bf16[256,1...) custom-call(f32[32,1024]{1,0:T(8,128)} %panel_ref.1, f32[2048,1024]{1,0:T(8,128)} %w_ref.1), custom_call_target="tpu_custom_call" | custom-call | tf_op jit(solution)/shard_map/gather_and_factor/pallas_call | solution.py:340
  81.5 0.0 copy-start
  81.6 0.0 copy-start.1
  81.6 11.9 %subtract.1 = f32[2048,1024]{1,0:T(8,128)} custom-call(f32[2048,1024]{1,0:T(8,128)} %w_ref.1, bf16[2048,256]{1,0:T(8,128)(2,1)} %get-tuple-element.11.ch_ref, bf16[2048,256]{1,0:T(8,128)(2,1)} %get-tuple-element.12.cl_ref, bf16[256,1024]{1,0:T(8,128)(2,1)} %get-tuple-element.13.bh_ref, bf16[256,1024]{1,0:T(8,128)(2,1)} %get-tuple-element.14.bl_ref), custom_call_target="tpu_custom_call" | custom-call | tf_op jit(solution)/shard_map/subtract/pallas_call | solution.py:385
  93.4 0.0 copy-done
  93.4 0.7 copy.7
  94.1 0.0 copy-done.1
  94.1 0.7 copy.8
Async XLA Ops:
  81.5 11.9 %copy-start = (f32[256,256]{1,0:T(8,128)S(1)}, f32[256,256]{1,0:T(8,128)}, u32[]{:S(2)}) copy-start(f32[256,256]{1,0:T(8,128)} %get-tuple-element.18) | copy-start | bytes 786436
  81.6 12.6 %copy-start.1 = (f32[128,256]{1,0:T(8,128)S(1)}, f32[128,256]{1,0:T(8,128)}, u32[]{:S(2)}) copy-start(f32[128,256]{1,0:T(8,128)} %get-tuple-element.19) | copy-start | bytes 393220

commit v2 on v1

--- a/solution.py
+++ b/solution.py
@@ -17,7 +17,8 @@
 CHUNKS = 2
 S1 = 256 // CHUNKS
 S2 = S1 // 4
-BLOCK = 32
+BLOCK = 64
+TILES = 8
 
 
 def dot_nt(a, b, precision=None):
@@ -44,9 +45,9 @@
 
 def body(
     panel_ref, w_hbm,
-    u_out, top_out, ch_out, cl_out, bh_out, bl_out,
-    w_ref, wh_ref, wl_ref, a_ref, ah_ref, al_ref, gx_ref, gy_ref, gz_ref, t_ref,
-    c_ref, f_ref, r1_ref, r2_ref, w_sem, send_sem, recv_sem,
+    u_out, top_out, w_ref, f_ref, bh_out, bl_out,
+    wh_ref, wl_ref, a_ref, ah_ref, al_ref, gx_ref, gy_ref, gz_ref, t_ref,
+    c_ref, r1_ref, r2_ref, w_sem, send_sem, recv_sem,
 ):
     row = lax.axis_index("row")
     col = lax.axis_index("col")
@@ -110,30 +111,42 @@
     def pass_on(index, who, h, dev):
         return send(index, a_ref.at[who, half[h]], a_ref.at[who, half[h]], dev)
 
+    gram_blocks = [None] * 4
+
+    def pair_here(d):
+        first = step(z, d) * 2
+        pair = a_ref[pl.ds(first, 2)].reshape(2 * PIECE, DEPTH)
+        where = pl.ds(pl.multiple_of(first * PIECE, 2 * PIECE), 2 * PIECE)
+        high, low = split(pair)
+        ah_ref[where, :] = high
+        al_ref[where, :] = low
+        gram_blocks[d] = dot_nt(panel_ref[...], pair, HIGHEST)
+
     own["up0"].wait_recv()
     relay0 = pass_on(5, below, 0, up)
     own["down1"].wait_recv()
     relay1 = pass_on(6, above, 1, down)
     forwards = [pass_on(7, below, 0, partner), pass_on(8, above, 1, partner)]
+    own["partner"].wait_recv()
+    pair_here(0)
     own["up1"].wait_recv()
     forwards.append(pass_on(9, below, 1, partner))
     own["down0"].wait_recv()
     forwards.append(pass_on(10, above, 0, partner))
+    for copy in forwards:
+        copy.wait_recv()
+    pair_here(1)
+    pair_here(3)
     relay0.wait_recv()
     forwards.append(pass_on(11, far, 0, partner))
     relay1.wait_recv()
     forwards.append(pass_on(12, far, 1, partner))
-    own["partner"].wait_recv()
-    for copy in forwards:
+    for copy in forwards[4:]:
         copy.wait_recv()
-
-    panel = a_ref[...].reshape(N, DEPTH)
-    high, low = split(panel)
-    ah_ref[...] = high
-    al_ref[...] = low
+    pair_here(2)
 
     base = N_PANEL
-    gx_ref[x] = dot_nt(panel_ref[...], panel, HIGHEST)
+    gx_ref[x] = pltpu.roll(jnp.concatenate(gram_blocks, axis=1), z * 2 * PIECE, 1)
     gram_x = [send(base + d - 1, gx_ref.at[x], gx_ref.at[x], at_x(d)) for d in (1, 2, 3)]
 
     def gram_to_y():
@@ -156,25 +169,39 @@
         cols_at = lax.broadcasted_iota(jnp.int32, (N, N), 1)
         t_ref[:, N:] = jnp.where(rows_at == cols_at, 1.0, 0.0).astype(F32)
 
-    def factor(b):
+    sub = lax.broadcasted_iota(jnp.int32, (BLOCK, 128), 0)
+    lane = lax.broadcasted_iota(jnp.int32, (BLOCK, 128), 1)
+    state = [None]
+
+    def pivots(b, first, last):
         lo = b * BLOCK
-        tile, shift = lo // 128 * 128, lo % 128
-        e = t_ref[lo:lo + BLOCK, tile:tile + 128]
-        if shift:
-            e = pltpu.roll(e, 128 - shift, 1)
-        sub = lax.broadcasted_iota(jnp.int32, (BLOCK, 128), 0)
-        lane = lax.broadcasted_iota(jnp.int32, (BLOCK, 128), 1)
-        e = jnp.where(lane < BLOCK, e, jnp.where(lane == sub + BLOCK, 1.0, 0.0).astype(F32))
-        for j in range(BLOCK - 1):
-            pivot_row = e[j:j + 1, :]
-            pivot = jnp.broadcast_to(pivot_row[:, j:j + 1], (1, 128))
-            column = jnp.broadcast_to(e[:, j:j + 1], (BLOCK, 128))
-            e = e - jnp.where(sub > j, column, 0.0) * (pivot_row / pivot)
+        if first == 0:
+            tile, shift = lo // 128 * 128, lo % 128
+            e = t_ref[lo:lo + BLOCK, tile:tile + 128]
+            if shift:
+                e = pltpu.roll(e, 128 - shift, 1)
+            e = jnp.where(lane < BLOCK, e, jnp.where(lane == sub + BLOCK, 1.0, 0.0).astype(F32))
+        else:
+            e = state[0]
+        for j in range(first, last, 2):
+            r0, r1 = e[j:j + 1, :], e[j + 1:j + 2, :]
+            c0 = jnp.broadcast_to(e[:, j:j + 1], (BLOCK, 128))
+            c1 = jnp.broadcast_to(e[:, j + 1:j + 2], (BLOCK, 128))
+            p, q, r = c0[j:j + 1, :], c1[j:j + 1, :], c1[j + 1:j + 2, :]
+            over = 1.0 / (p * r - q * q)
+            w0, w1 = (r * r0 - q * r1) * over, (p * r1 - q * r0) * over
+            change = jnp.where(sub > j + 1, c0 * w0 + c1 * w1, 0.0)
+            change = jnp.where(sub == j + 1, q * (r0 / p), change)
+            e = e - change
+        state[0] = e
+
+    def apply(b):
+        lo = b * BLOCK
+        e = state[0]
         diagonal = jnp.sum(jnp.where(lane == sub, e, 0.0), axis=1, keepdims=True)
         root = lax.rsqrt(diagonal)
         root = root * (1.5 - 0.5 * diagonal * root * root)
-        e = e * root
-        inverse = e[:, BLOCK:2 * BLOCK]
+        inverse = (e * root)[:, BLOCK:2 * BLOCK]
         done = dot_nn(inverse, t_ref[lo:lo + BLOCK, :], HIGHEST)
         t_ref[lo:lo + BLOCK, :] = done
         if lo + BLOCK < N:
@@ -189,9 +216,13 @@
         t_ref[:, N:] = inverse
         q = dot_nn(inverse, a_ref[...].reshape(N, DEPTH), HIGHEST)
         high, low = split(dot_tn(inverse, q, HIGHEST))
-        bh_ref, bl_ref = bh_out, bl_out
-        bh_ref[...] = high
-        bl_ref[...] = low
+        bh_out[...] = high
+        bl_out[...] = low
+
+    pieces = []
+    for b in range(N // BLOCK):
+        pieces.append(lambda b=b: pivots(b, 0, BLOCK // 2))
+        pieces.append(lambda b=b: (pivots(b, BLOCK // 2, BLOCK), apply(b)))
 
     def rows_of(start, size, align):
         return pl.ds(pl.multiple_of(start, align), size)
@@ -312,22 +343,16 @@
     product(1, 0)
     run(0, 2)
     gram_done(gram_z)
-    factor(0)
+    pieces[0]()
     run(1, 2)
     for number in range(3, 9):
         run(0, number)
-        factor(number - 2)
+        pieces[number - 2]()
         run(1, number)
-    factor(7)
+    pieces[7]()
     run(0, 9)
     finish()
     run(1, 9)
-
-    for b in range(8):
-        rows = pl.ds(b * 256, 256)
-        high, low = split(f_ref[rows, :])
-        ch_out[rows, :] = high
-        cl_out[rows, :] = low
     top_out[...] = dot_nt(f_ref[rows_of(row * 128, 128, 128), :], t_ref[:, N:], HIGHEST)
 
     for copy in sent:
@@ -340,17 +365,16 @@
     return pl.pallas_call(
         body,
         out_shape=(
-            jax.ShapeDtypeStruct((N, N), F32),
-            jax.ShapeDtypeStruct((128, N), F32),
-            jax.ShapeDtypeStruct((SLAB, N), BF16),
-            jax.ShapeDtypeStruct((SLAB, N), BF16),
-            jax.ShapeDtypeStruct((N, DEPTH), BF16),
-            jax.ShapeDtypeStruct((N, DEPTH), BF16),
+            pltpu.VMEM((N, N), F32),
+            pltpu.VMEM((128, N), F32),
+            pltpu.VMEM((SLAB, DEPTH), F32),
+            pltpu.VMEM((SLAB, N), F32),
+            pltpu.VMEM((N, DEPTH), BF16),
+            pltpu.VMEM((N, DEPTH), BF16),
         ),
         in_specs=[vmem, pl.BlockSpec(memory_space=pl.ANY)],
         out_specs=(vmem,) * 6,
         scratch_shapes=[
-            pltpu.VMEM((SLAB, DEPTH), F32),
             pltpu.VMEM((SLAB, DEPTH), BF16),
             pltpu.VMEM((SLAB, DEPTH), BF16),
             pltpu.VMEM((8, PIECE, DEPTH), F32),
@@ -361,7 +385,6 @@
             pltpu.VMEM((8, PIECE, N), F32),
             pltpu.VMEM((N, 2 * N), F32),
             pltpu.VMEM((SLAB, N), F32),
-            pltpu.VMEM((SLAB, N), F32),
             pltpu.VMEM((2, CHUNKS, 6, S1 // 2, N), F32),
             pltpu.VMEM((2, CHUNKS, 6, S2 // 2, N), F32),
             pltpu.SemaphoreType.DMA((8,)),
@@ -369,39 +392,56 @@
             pltpu.SemaphoreType.DMA((count,)),
         ],
         compiler_params=pltpu.CompilerParams(
-            collective_id=0, has_side_effects=True, vmem_limit_bytes=56 * 2**20
+            collective_id=0, has_side_effects=True, vmem_limit_bytes=36 * 2**20
         ),
         name="gather_and_factor",
     )(panel_cols, window_cols)
 
 
-def residual_body(w_ref, ch_ref, cl_ref, bh_ref, bl_ref, out_ref):
-    ch, cl, bh, bl = ch_ref[...], cl_ref[...], bh_ref[...], bl_ref[...]
-    out_ref[...] = w_ref[...] - ((dot_nn(ch, bl) + dot_nn(cl, bh)) + dot_nn(ch, bh))
-
-
-def subtract(window_cols, ch, cl, bh, bl):
-    rows = 256
+def subtract_body(u_ref, top_ref, w_ref, f_ref, bh_ref, bl_ref, u_out, top_out, out, r_ref, sem, side_sem):
+    sides = [
+        pltpu.make_async_copy(u_ref, u_out, side_sem.at[0]),
+        pltpu.make_async_copy(top_ref, top_out, side_sem.at[1]),
+    ]
+    for copy in sides:
+        copy.start()
+    rows = SLAB // TILES
+    copies = []
+    for b in range(TILES):
+        where = pl.ds(b * rows, rows)
+        fh, fl = split(f_ref[where, :])
+        bh = bh_ref[...]
+        r_ref[where, :] = w_ref[where, :] - ((dot_nn(fh, bl_ref[...]) + dot_nn(fl, bh)) + dot_nn(fh, bh))
+        copies.append(pltpu.make_async_copy(r_ref.at[where, :], out.at[where, :], sem.at[b]))
+        copies[-1].start()
+    for copy in sides + copies:
+        copy.wait()
+
+
+def subtract(*given):
+    vmem = pl.BlockSpec(memory_space=pltpu.VMEM)
+    anywhere = pl.BlockSpec(memory_space=pl.ANY)
     return pl.pallas_call(
-        residual_body,
-        out_shape=jax.ShapeDtypeStruct((SLAB, DEPTH), F32),
-        grid=(SLAB // rows,),
-        in_specs=[
-            pl.BlockSpec((rows, DEPTH), lambda i: (i, 0)),
-            pl.BlockSpec((rows, N), lambda i: (i, 0)),
-            pl.BlockSpec((rows, N), lambda i: (i, 0)),
-            pl.BlockSpec((N, DEPTH), lambda i: (0, 0)),
-            pl.BlockSpec((N, DEPTH), lambda i: (0, 0)),
+        subtract_body,
+        out_shape=(
+            jax.ShapeDtypeStruct((N, N), F32),
+            jax.ShapeDtypeStruct((128, N), F32),
+            jax.ShapeDtypeStruct((SLAB, DEPTH), F32),
+        ),
+        in_specs=[vmem] * 6,
+        out_specs=(anywhere,) * 3,
+        scratch_shapes=[
+            pltpu.VMEM((SLAB, DEPTH), F32),
+            pltpu.SemaphoreType.DMA((TILES,)),
+            pltpu.SemaphoreType.DMA((2,)),
         ],
-        out_specs=pl.BlockSpec((rows, DEPTH), lambda i: (i, 0)),
+        compiler_params=pltpu.CompilerParams(vmem_limit_bytes=24 * 2**20),
         name="subtract",
-    )(window_cols, ch, cl, bh, bl)
+    )(*given)
 
 
 def local(panel_cols, window_cols):
-    triangle, top_rows, ch, cl, bh, bl = gather_and_factor(panel_cols, window_cols)
-    residual = subtract(window_cols, ch, cl, bh, bl)
-    return triangle, top_rows, residual
+    return subtract(*gather_and_factor(panel_cols, window_cols))
 
 
 def solution(mesh):

time: 95.8 us -> 72.9 us (0.76)
  Pallas kernels: 92.8 us -> 71 us
    pallas_call x2, Pallas kernels: 92.8 us -> 71 us  [the longest x1 66.5 us: gather_and_factor(): pl.pallas_call(body, out_shape=(pltpu.VMEM((N, N), F32), pltpu.VMEM((128,...]
where the time goes in v2:
time: 72.9 us; the launch traced here: 72.7 us
  Pallas kernels  71 us (97%)
  local copies, waits for them, and re-layouts  0.9 us (1%)
  between operations  0.81 us (1%)
    pallas_call x1, Pallas kernels, gather_and_factor(): pl.pallas_call(body, out_shape=(pltpu.VMEM((N, N), F32), pltpu.VMEM((128,...  66.5 us
    pallas_call x1, Pallas kernels, subtract(): pl.pallas_call(subtract_body, out_shape=(jax.ShapeDtypeStruct((N, N), F32...  4.52 us

profile of v2, /device:TPU:0, one launch (start us, length us, event | category | flops | bytes accessed | tf_op | source)
XLA Modules:
  0.0 72.7 jit_solution(14798447364966267194)
XLA Ops:
  0.6 0.0 copy-start
  0.6 0.9 %copy-done = f32[32,1024]{1,0:T(8,128)S(1)} copy-done((f32[32,1024]{1,0:T(8,128)S(1)}, f32[32,1024]{1,0:T(8,128)}, u32[]{:S(2)}) %copy-start) | copy-done | bytes 131096
  1.5 66.5 %gather_and_factor.1 = (f32[256,256]{1,0:T(8,128)S(1)}, f32[128,256]{1,0:T(8,128)S(1)}, f32[2048,1024]{1,0:T(8,128)S(1)}, f32[2048,256]{1,0:T(8,128)S(1)}, bf16[...) custom-call(f32[32,1024]{1,0:T(8,128)S(1)} %copy-done, f32[2048,1024]{1,0:T(8,128)} %w_hbm.1), custom_call_target="tpu_custom_call" | custom-call | tf_op jit(solution)/shard_map/gather_and_factor/pallas_call | solution.py:365
  68.1 4.5 %subtract.1 = (f32[256,256]{1,0:T(8,128)}, f32[128,256]{1,0:T(8,128)}, f32[2048,1024]{1,0:T(8,128)}) custom-call(f32[256,256]{1,0:T(8,128)S(1)} %get-tuple-element.9.u_ref, f32[128,256]{1,0:T(8,128)S(1)} %get-tuple-element.10.top_ref, f32[2048,1024]{1,0:T(8,128)S(1)} %get-tuple-element.11.w_ref, f32[2048,256]{1,0:T(8,128)S(1)} %get-tuple-element.12.f_ref, ...), custom_call_target="tpu_custom_call" | custom-call | tf_op jit(solution)/shard_map/subtract/pallas_call | solution.py:424
Async XLA Ops:
  0.6 0.9 %copy-start = (f32[32,1024]{1,0:T(8,128)S(1)}, f32[32,1024]{1,0:T(8,128)}, u32[]{:S(2)}) copy-start(f32[32,1024]{1,0:T(8,128)} %panel_ref.1) | copy-start | bytes 393220

commit v3 on v2

v3 whole, which is shorter than its diff:
```python
import jax
import jax.numpy as jnp
from jax import lax
from jax.experimental import pallas as pl
from jax.experimental.pallas import tpu as pltpu
from jax.sharding import PartitionSpec as P

MESH = pl.DeviceIdType.MESH
HIGHEST = lax.Precision.HIGHEST
F32 = jnp.float32
BF16 = jnp.bfloat16

N = 256
SLAB = 2048
DEPTH = 1024
PIECE = 32
HALF = 128
CHUNKS = 2
S1 = 256 // CHUNKS
S2 = S1 // 4
BLOCK = 64
TILES = 8


def dot_nt(a, b, precision=None):
    return lax.dot_general(a, b, (((1,), (1,)), ((), ())), precision=precision, preferred_element_type=F32)


def dot_nn(a, b, precision=None):
    return lax.dot_general(a, b, (((1,), (0,)), ((), ())), precision=precision, preferred_element_type=F32)


def dot_tn(a, b, precision=None):
    return lax.dot_general(a, b, (((0,), (0,)), ((), ())), precision=precision, preferred_element_type=F32)


def split(v):
    high = v.astype(BF16)
    return high, (v - high.astype(F32)).astype(BF16)


def spread_row(v, r):
    return jnp.broadcast_to(v[r:r + 1, :], (8, 128))


def spread_lane(v, c):
    return jnp.broadcast_to(v[:, c:c + 1], (8, 128))


def eliminate(groups, g):
    sub = lax.broadcasted_iota(jnp.int32, (8, 128), 0)
    v = groups[g]
    c = [spread_lane(v, 8 * g + t) for t in range(8)]
    w, m = [None] * 8, {}
    for t in range(0, 8, 2):
        r0, r1 = spread_row(v, t), spread_row(v, t + 1)
        p, q, r = spread_row(c[t], t), spread_row(c[t + 1], t), spread_row(c[t + 1], t + 1)
        over = 1.0 / (p * r - q * q)
        po, qo, ro = p * over, q * over, r * over
        w[t], w[t + 1] = ro * r0 - qo * r1, po * r1 - qo * r0
        for u in range(t + 2, 8):
            pu, su = spread_row(c[u], t), spread_row(c[u], t + 1)
            m[t, u], m[t + 1, u] = ro * pu - qo * su, po * su - qo * pu
            c[u] = c[u] - (c[t] * m[t, u] + c[t + 1] * m[t + 1, u])
        new = v - (c[t] * w[t] + c[t + 1] * w[t + 1])
        v = jnp.where(sub > t + 1, new, jnp.where(sub == t + 1, r1 - (q / p) * r0, v))
    groups[g] = v
    if g + 1 == len(groups):
        return
    solved = list(w)
    for t in (4, 2, 0):
        for s in (t, t + 1):
            total = m[s, t + 2] * solved[t + 2]
            for u in range(t + 3, 8):
                total = total + m[s, u] * solved[u]
            solved[s] = w[s] - total
    for i in range(g + 1, len(groups)):
        p = [spread_lane(groups[i], 8 * g + t) * solved[t] for t in range(8)]
        groups[i] = groups[i] - (((p[0] + p[1]) + (p[2] + p[3])) + ((p[4] + p[5]) + (p[6] + p[7])))


N_PANEL = 13
N_GRAM = 19
N_CROSS = 4 * CHUNKS * 24


def body(
    panel_hbm, w_hbm,
    u_out, inv_out, w_ref, f_ref, bh_out, bl_out,
    panel_ref, wh_ref, wl_ref, a_ref, ab_ref, g1_ref, g2_ref, gz_ref, t_ref,
    c_ref, r1_ref, r2_ref, w_sem, send_sem, recv_sem,
):
    row = lax.axis_index("row")
    col = lax.axis_index("col")
    y, x = lax.div(row, 4), lax.rem(row, 4)
    z, k = lax.div(col, 2), lax.rem(col, 2)

    def step(v, d):
        return lax.rem(v + d, 4)

    def at_x(d):
        return (y * 4 + step(x, d), col)

    def at_y(d):
        return (step(y, d) * 4 + x, col)

    def piece(d, core):
        return step(z, d) * 2 + core

    def at_z(d):
        return (row, piece(d, k))

    partner = (row, z * 2 + 1 - k)

    def load_window(b):
        where = pl.ds(b * 256, 256)
        return pltpu.make_async_copy(w_hbm.at[where, :], w_ref.at[where, :], w_sem.at[b])

    load_panel = pltpu.make_async_copy(panel_hbm, panel_ref, w_sem.at[8])
    load_panel.start()
    for b in range(8):
        load_window(b).start()

    barrier = pltpu.get_barrier_semaphore()
    others = [at_x(d) for d in (1, 2, 3)] + [at_y(d) for d in (1, 2, 3)] + [at_z(d) for d in (1, 2, 3)] + [partner]
    for dev in others:
        pl.semaphore_signal(barrier, inc=1, device_id=dev, device_id_type=MESH)
    load_panel.wait()
    pl.semaphore_wait(barrier, len(others))

    sent = []

    def send(index, src, dst, dev):
        copy = pltpu.make_async_remote_copy(
            src_ref=src, dst_ref=dst, send_sem=send_sem.at[index], recv_sem=recv_sem.at[index],
            device_id=dev, device_id_type=MESH,
        )
        copy.start()
        sent.append(copy)
        return copy

    half = (pl.ds(0, 16), pl.ds(16, 16))
    up, down = at_z(1), at_z(3)
    own = {}
    own["up0"] = send(0, panel_ref.at[half[0]], a_ref.at[col, half[0]], up)
    own["down1"] = send(1, panel_ref.at[half[1]], a_ref.at[col, half[1]], down)
    own["up1"] = send(2, panel_ref.at[half[1]], a_ref.at[col, half[1]], up)
    own["down0"] = send(3, panel_ref.at[half[0]], a_ref.at[col, half[0]], down)
    own["partner"] = send(4, panel_ref, a_ref.at[col], partner)
    a_ref[col] = panel_ref[...]

    def split_window(first, last):
        for b in range(first, last):
            rows = pl.ds(b * 256, 256)
            load_window(b).wait()
            high, low = split(w_ref[rows, :])
            wh_ref[rows, :] = high
            wl_ref[rows, :] = low

    below, above, far = piece(3, k), piece(1, k), piece(2, k)
    gram_blocks = [None] * 4

    def pass_on(index, who, h, dev):
        return send(index, a_ref.at[who, half[h]], a_ref.at[who, half[h]], dev)

    def pair_here(d):
        pair = a_ref[pl.ds(step(z, d) * 2, 2)].reshape(2 * PIECE, DEPTH)
        high, low = split(pair)
        ab_ref[d // 2, pl.ds(d % 2 * 64, 64), :] = high
        ab_ref[d // 2, pl.ds(HALF + d % 2 * 64, 64), :] = low
        gram_blocks[d] = dot_nt(panel_ref[...], pair, HIGHEST)

    split_window(0, 5)
    own["down1"].wait_recv()
    relay1 = pass_on(6, above, 1, down)
    forward_above = [pass_on(8, above, 1, partner)]
    own["up0"].wait_recv()
    relay0 = pass_on(5, below, 0, up)
    forward_below = [pass_on(7, below, 0, partner)]
    split_window(5, 8)
    own["partner"].wait_recv()
    pair_here(0)
    own["down0"].wait_recv()
    forward_above.append(pass_on(10, above, 0, partner))
    own["up1"].wait_recv()
    forward_below.append(pass_on(9, below, 1, partner))
    for copy in forward_above:
        copy.wait_recv()
    pair_here(1)

    def gram_start():
        slab = pltpu.roll(jnp.concatenate(gram_blocks, axis=1), z * 2 * PIECE, 1)
        copies = []
        for part, (me, at) in enumerate(((x, at_x), (y, at_y))):
            g1_ref[part, me] = slab[part * 16:part * 16 + 16, :]
            copies += [
                send(N_PANEL + part * 3 + d - 1, g1_ref.at[part, me], g1_ref.at[part, me], at(d)) for d in (1, 2, 3)
            ]
        return copies

    def summed(ref, part):
        return (ref[part, 0] + ref[part, 1]) + (ref[part, 2] + ref[part, 3])

    def gram_turn(arriving):
        copies = []
        for part, (me, at) in enumerate(((y, at_y), (x, at_x))):
            for copy in arriving[part * 3:part * 3 + 3]:
                copy.wait_recv()
            g2_ref[part, me] = summed(g1_ref, part)
            copies += [
                send(N_PANEL + 6 + part * 3 + d - 1, g2_ref.at[part, me], g2_ref.at[part, me], at(d)) for d in (1, 2, 3)
            ]
        return copies

    def gram_to_col(arriving):
        for part in range(2):
            for copy in arriving[part * 3:part * 3 + 3]:
                copy.wait_recv()
            gz_ref[col, part * 16:part * 16 + 16] = summed(g2_ref, part)
        copies = [send(N_PANEL + 12 + d - 1, gz_ref.at[col], gz_ref.at[col], at_z(d)) for d in (1, 3, 2)]
        return copies + [send(N_PANEL + 15, gz_ref.at[col], gz_ref.at[col], partner)]

    def gram_done(arriving):
        forwards = []
        for n, d in enumerate((3, 1, 2)):
            arriving[n].wait_recv()
            there = gz_ref.at[piece(d, k)]
            forwards.append(send(N_PANEL + 16 + n, there, there, partner))
        arriving[3].wait_recv()
        for copy in forwards:
            copy.wait_recv()
        t_ref[:, :N] = gz_ref[...].reshape(N, N)
        rows_at = lax.broadcasted_iota(jnp.int32, (N, N), 0)
        cols_at = lax.broadcasted_iota(jnp.int32, (N, N), 1)
        t_ref[:, N:] = jnp.where(rows_at == cols_at, 1.0, 0.0).astype(F32)

    sub = lax.broadcasted_iota(jnp.int32, (BLOCK, 128), 0)
    lane = lax.broadcasted_iota(jnp.int32, (BLOCK, 128), 1)
    groups = []

    def tile_of(lo, at):
        e = t_ref[lo:lo + BLOCK, at // 128 * 128:at // 128 * 128 + 128]
        return pltpu.roll(e, 128 - at % 128, 1) if at % 128 else e

    def begin(e):
        e = jnp.where(lane < BLOCK, e, jnp.where(lane == sub + BLOCK, 1.0, 0.0).astype(F32))
        groups[:] = [e[8 * i:8 * i + 8, :] for i in range(BLOCK // 8)]

    def apply(b):
        lo, hi = b * BLOCK, b * BLOCK + BLOCK
        e = jnp.concatenate(groups, axis=0)
        diagonal = jnp.sum(jnp.where(lane == sub, e, 0.0), axis=1, keepdims=True)
        root = lax.rsqrt(diagonal)
        root = root * (1.5 - 0.5 * diagonal * root * root)
        inverse = (e * root)[:, BLOCK:2 * BLOCK]
        if hi < N:
            ahead = dot_nn(inverse, tile_of(lo, hi), HIGHEST)
            begin(tile_of(hi, hi) - dot_tn(ahead[:, :BLOCK], ahead, HIGHEST))
        done = dot_nn(inverse, t_ref[lo:lo + BLOCK, :], HIGHEST)
        t_ref[lo:lo + BLOCK, :] = done
        if hi < N:
            update = dot_tn(done[:, :N], done, HIGHEST)
            t_ref[hi:, :] -= update[hi:, :]

    def finish():
        rows_at = lax.broadcasted_iota(jnp.int32, (N, N), 0)
        cols_at = lax.broadcasted_iota(jnp.int32, (N, N), 1)
        u_out[...] = jnp.where(cols_at >= rows_at, t_ref[:, :N], 0.0)
        inverse = jnp.where(cols_at <= rows_at, t_ref[:, N:], 0.0)
        inverse = pltpu.roll(inverse, lax.rem(4 - z, 4) * 2 * PIECE, 1)
        inv_out[...] = inverse
        ih, il = split(inverse)
        ah = jnp.concatenate([ab_ref[0, :HALF, :], ab_ref[1, :HALF, :]], axis=0)
        al = jnp.concatenate([ab_ref[0, HALF:, :], ab_ref[1, HALF:, :]], axis=0)
        qh, ql = split((dot_nn(ih, al) + dot_nn(il, ah)) + dot_nn(ih, ah))
        high, low = split((dot_tn(ih, ql) + dot_tn(il, qh)) + dot_tn(ih, qh))
        bh_out[...] = high
        bl_out[...] = low

    def pieces():
        begin(tile_of(0, 0))
        for b in range(N // BLOCK):
            for g in range(BLOCK // 8):
                eliminate(groups, g)
                if g in (1, 3, 5):
                    yield
            apply(b)

    def rows_of(start, size, align):
        return pl.ds(pl.multiple_of(start, align), size)

    def product(h, d):
        for part in range(2):
            where = rows_of(part * 1024 + step(y if part else x, d) * 256, 256, 256)
            both = dot_nt(wh_ref[where, :], ab_ref[h])
            low = dot_nt(wl_ref[where, :], ab_ref[h, :HALF, :])
            c_ref[h, where, :] = (both[:, HALF:] + low) + both[:, :HALF]

    class Stream:
        def __init__(self, h, chunk, part):
            self.h = h
            self.at = (at_y, at_x) if part else (at_x, at_y)
            self.me = (y, x) if part else (x, y)
            self.start = part * 1024 + chunk * S1
            number = (h * CHUNKS + chunk) * 2 + part
            self.index = N_PANEL + N_GRAM + number * 24
            self.buf = (r1_ref.at[number], r2_ref.at[number])

        def place(self, axis, d, h):
            size = S2 if axis else S1
            if axis:
                start = self.start + self.me[0] * 256 + step(self.me[1], d) * S2
            else:
                start = self.start + step(self.me[0], d) * 256
            return rows_of(start + h * (size // 2), size // 2, size // 2)

        def rs_send(self, axis, slot, src, d):
            return send(self.index + axis * 6 + slot, c_ref.at[self.h, src, :], self.buf[axis].at[slot], self.at[axis](d))

        def far_out(self, axis):
            self.rs = [None] * 6
            self.rs[0] = self.rs_send(axis, 0, self.place(axis, 2, 0), 1)
            self.rs[1] = self.rs_send(axis, 1, self.place(axis, 2, 1), 3)

        def near_out(self, axis):
            self.rs[2] = self.rs_send(axis, 2, self.place(axis, 1, 1), 1)
            self.rs[3] = self.rs_send(axis, 3, self.place(axis, 3, 0), 3)

        def relay(self, axis):
            for slot, (d, h) in enumerate(((1, 0), (3, 1))):
                self.rs[slot].wait_recv()
                where = self.place(axis, d, h)
                c_ref[self.h, where, :] += self.buf[axis][slot]
                self.rs[4 + slot] = self.rs_send(axis, 4 + slot, where, d)

        def gathered(self, axis, into):
            for slot in (2, 3, 4, 5):
                self.rs[slot].wait_recv()
            for h, (a, b) in enumerate(((3, 4), (2, 5))):
                where = self.place(axis, 0, h)
                into[self.h, where, :] = c_ref[self.h, where, :] + (self.buf[axis][a] + self.buf[axis][b])

        def ag_send(self, axis, slot, where, d):
            there = f_ref.at[self.h, where, :]
            return send(self.index + 12 + axis * 6 + slot, there, there, self.at[axis](d))

        def spread(self, axis):
            self.ag = [
                self.ag_send(axis, 0, self.place(axis, 0, 0), 1),
                self.ag_send(axis, 1, self.place(axis, 0, 1), 3),
                self.ag_send(axis, 2, self.place(axis, 0, 1), 1),
                self.ag_send(axis, 3, self.place(axis, 0, 0), 3),
            ]

        def hand_on(self, axis):
            self.ag[0].wait_recv()
            self.ag.append(self.ag_send(axis, 4, self.place(axis, 3, 0), 1))
            self.ag[1].wait_recv()
            self.ag.append(self.ag_send(axis, 5, self.place(axis, 1, 1), 3))

        def spread_done(self, axis):
            for slot in (2, 3, 4, 5):
                self.ag[slot].wait_recv()

    streams = [[Stream(h, chunk, part) for part in range(2)] for h in range(2) for chunk in range(CHUNKS)]

    def run(number, *which):
        for n in which:
            for s in streams[n]:
                if number == 0:
                    s.far_out(0)
                elif number == 1:
                    s.near_out(0)
                elif number == 2:
                    s.relay(0)
                elif number == 3:
                    s.gathered(0, c_ref)
                    s.far_out(1)
                    s.near_out(1)
                elif number == 4:
                    s.relay(1)
                elif number == 5:
                    s.gathered(1, f_ref)
                    s.spread(1)
                elif number == 6:
                    s.hand_on(1)
                elif number == 7:
                    s.spread_done(1)
                    s.spread(0)
                elif number == 8:
                    s.hand_on(0)
                elif number == 9:
                    s.spread_done(0)

    product(0, 2)
    run(0, 0, 1)
    product(0, 1)
    product(0, 3)
    for copy in forward_below:
        copy.wait_recv()
    pair_here(3)
    relay0.wait_recv()
    forward_far = [pass_on(11, far, 0, partner)]
    relay1.wait_recv()
    forward_far.append(pass_on(12, far, 1, partner))
    run(1, 0, 1)
    product(0, 0)
    for copy in forward_far:
        copy.wait_recv()
    pair_here(2)
    gram = gram_start()
    run(2, 0, 1)
    product(1, 2)
    run(0, 2, 3)
    gram = gram_turn(gram)
    run(3, 0, 1)
    product(1, 1)
    product(1, 3)
    run(1, 2, 3)
    gram = gram_to_col(gram)
    product(1, 0)
    run(2, 2, 3)
    run(4, 0, 1)
    run(3, 2, 3)
    run(5, 0, 1)
    gram_done(gram)
    work = pieces()
    plan = (
        (), ((6, 0, 1), (4, 2, 3)), ((7, 0, 1),), ((5, 2, 3),), ((8, 0, 1),), ((6, 2, 3),), ((9, 0, 1),),
        ((7, 2, 3),), (), ((8, 2, 3),), (), (),
    )
    for rounds in plan:
        for number, *which in rounds:
            run(number, *which)
        next(work, None)
    for _ in work:
        pass
    finish()
    run(9, 2, 3)

    for copy in sent:
        copy.wait_send()


def gather_and_factor(panel_cols, window_cols):
    vmem = pl.BlockSpec(memory_space=pltpu.VMEM)
    count = N_PANEL + N_GRAM + N_CROSS
    return pl.pallas_call(
        body,
        out_shape=(
            pltpu.VMEM((N, N), F32),
            pltpu.VMEM((N, N), F32),
            pltpu.VMEM((SLAB, DEPTH), F32),
            pltpu.VMEM((2, SLAB, HALF), F32),
            pltpu.VMEM((N, DEPTH), BF16),
            pltpu.VMEM((N, DEPTH), BF16),
        ),
        in_specs=[pl.BlockSpec(memory_space=pltpu.HBM)] * 2,
        out_specs=(vmem,) * 6,
        scratch_shapes=[
            pltpu.VMEM((PIECE, DEPTH), F32),
            pltpu.VMEM((SLAB, DEPTH), BF16),
            pltpu.VMEM((SLAB, DEPTH), BF16),
            pltpu.VMEM((8, PIECE, DEPTH), F32),
            pltpu.VMEM((2, 2 * HALF, DEPTH), BF16),
            pltpu.VMEM((2, 4, 16, N), F32),
            pltpu.VMEM((2, 4, 16, N), F32),
            pltpu.VMEM((8, PIECE, N), F32),
            pltpu.VMEM((N, 2 * N), F32),
            pltpu.VMEM((2, SLAB, HALF), F32),
            pltpu.VMEM((4 * CHUNKS, 6, S1 // 2, HALF), F32),
            pltpu.VMEM((4 * CHUNKS, 6, S2 // 2, HALF), F32),
            pltpu.SemaphoreType.DMA((9,)),
            pltpu.SemaphoreType.DMA((count,)),
            pltpu.SemaphoreType.DMA((count,)),
        ],
        compiler_params=pltpu.CompilerParams(
            collective_id=0, has_side_effects=True, vmem_limit_bytes=36 * 2**20
        ),
        name="gather_and_factor",
    )(panel_cols, window_cols)


def subtract_body(u_ref, inv_ref, w_ref, f_ref, bh_ref, bl_ref, u_out, top_out, out, r_ref, top_ref, sem):
    copies = [pltpu.make_async_copy(u_ref, u_out, sem.at[TILES])]
    copies[0].start()
    rows = SLAB // TILES
    for b in range(TILES):
        where = pl.ds(b * rows, rows)
        fh, fl = split(jnp.concatenate([f_ref[0, where, :], f_ref[1, where, :]], axis=1))
        bh = bh_ref[...]
        r_ref[where, :] = w_ref[where, :] - ((dot_nn(fh, bl_ref[...]) + dot_nn(fl, bh)) + dot_nn(fh, bh))
        copies.append(pltpu.make_async_copy(r_ref.at[where, :], out.at[where, :], sem.at[b]))
        copies[-1].start()
        if b == TILES - 2:
            mine = pl.ds(pl.multiple_of(lax.axis_index("row") * 128, 128), 128)
            share = jnp.concatenate([f_ref[0, mine, :], f_ref[1, mine, :]], axis=1)
            top_ref[...] = dot_nt(share, inv_ref[...], HIGHEST)
            copies.append(pltpu.make_async_copy(top_ref, top_out, sem.at[TILES + 1]))
            copies[-1].start()
    for copy in copies:
        copy.wait()


def subtract(*given):
    vmem = pl.BlockSpec(memory_space=pltpu.VMEM)
    anywhere = pl.BlockSpec(memory_space=pl.ANY)
    return pl.pallas_call(
        subtract_body,
        out_shape=(
            jax.ShapeDtypeStruct((N, N), F32),
            jax.ShapeDtypeStruct((128, N), F32),
            jax.ShapeDtypeStruct((SLAB, DEPTH), F32),
        ),
        in_specs=[vmem] * 6,
        out_specs=(anywhere,) * 3,
        scratch_shapes=[
            pltpu.VMEM((SLAB, DEPTH), F32),
            pltpu.VMEM((128, N), F32),
            pltpu.SemaphoreType.DMA((TILES + 2,)),
        ],
        compiler_params=pltpu.CompilerParams(vmem_limit_bytes=24 * 2**20),
        name="subtract",
    )(*given)


def local(panel_cols, window_cols):
    return subtract(*gather_and_factor(panel_cols, window_cols))


def solution(mesh):
    return jax.shard_map(
        local,
        mesh=mesh,
        in_specs=(P("col", "row"), P("col", "row")),
        out_specs=(P(), P(("col", "row"), None), P("col", "row")),
        check_vma=False,
    )
```

time: 72.9 us -> 68.3 us (0.937)
  Pallas kernels: 71 us -> 66.5 us
    pallas_call x1, Pallas kernels: 66.5 us -> 61.2 us  [gather_and_factor(): pl.pallas_call(body, out_shape=(pltpu.VMEM((N, N), F32), pltpu.VMEM((N, N...]
    pallas_call x1, Pallas kernels: 4.52 us -> 5.26 us  [subtract(): pl.pallas_call(subtract_body, out_shape=(jax.ShapeDtypeStruct((N, N), F32...]
where the time goes in v3:
time: 68.3 us; the launch traced here: 68.2 us
  Pallas kernels  66.5 us (97%)
  local copies, waits for them, and re-layouts  0.9 us (1%)
  between operations  0.81 us (1%)
    pallas_call x1, Pallas kernels, gather_and_factor(): pl.pallas_call(body, out_shape=(pltpu.VMEM((N, N), F32), pltpu.VMEM((N, N...  61.2 us
    pallas_call x1, Pallas kernels, subtract(): pl.pallas_call(subtract_body, out_shape=(jax.ShapeDtypeStruct((N, N), F32...  5.26 us

profile of v3, /device:TPU:0, one launch (start us, length us, event | category | flops | bytes accessed | tf_op | source)
XLA Modules:
  0.0 68.2 jit_solution(16942488995696313947)
XLA Ops:
  0.6 0.0 copy-start
  0.6 0.9 %copy-done = f32[32,1024]{1,0:T(8,128)S(1)} copy-done((f32[32,1024]{1,0:T(8,128)S(1)}, f32[32,1024]{1,0:T(8,128)}, u32[]{:S(2)}) %copy-start) | copy-done | bytes 131096
  1.5 61.2 %gather_and_factor.1 = (f32[256,256]{1,0:T(8,128)S(1)}, f32[256,256]{1,0:T(8,128)S(1)}, f32[2048,1024]{1,0:T(8,128)S(1)}, f32[2,2048,128]{2,1,0:T(8,128)S(1)}, b...) custom-call(f32[32,1024]{1,0:T(8,128)S(1)} %copy-done, f32[2048,1024]{1,0:T(8,128)} %w_hbm.1), custom_call_target="tpu_custom_call" | custom-call | tf_op jit(solution)/shard_map/gather_and_factor/pallas_call | solution.py:448
  62.8 5.3 %subtract.1 = (f32[256,256]{1,0:T(8,128)}, f32[128,256]{1,0:T(8,128)}, f32[2048,1024]{1,0:T(8,128)}) custom-call(f32[256,256]{1,0:T(8,128)S(1)} %get-tuple-element.9.u_ref, f32[256,256]{1,0:T(8,128)S(1)} %get-tuple-element.10.inv_ref, f32[2048,1024]{1,0:T(8,128)S(1)} %get-tuple-element.11.w_ref, f32[2,2048,128]{2,1,0:T(8,128)S(1)} %get-tuple-element.12.f_ref, ...), custom_call_target="tpu_custom_call" | custom-call | tf_op jit(solution)/shard_map/subtract/pallas_call | solution.py:508
Async XLA Ops:
  0.6 0.9 %copy-start = (f32[32,1024]{1,0:T(8,128)S(1)}, f32[32,1024]{1,0:T(8,128)}, u32[]{:S(2)}) copy-start(f32[32,1024]{1,0:T(8,128)} %panel_hbm.1) | copy-start | bytes 393220

commit v4 on v3

v4 whole, which is shorter than its diff:
```python
import jax
import jax.numpy as jnp
from jax import lax
from jax.experimental import pallas as pl
from jax.experimental.pallas import tpu as pltpu
from jax.sharding import PartitionSpec as P

MESH = pl.DeviceIdType.MESH
HIGHEST = lax.Precision.HIGHEST
F32 = jnp.float32
BF16 = jnp.bfloat16

N = 256
SLAB = 2048
DEPTH = 1024
PIECE = 32
HALF = 128
CHUNKS = 1
S1 = 256 // CHUNKS
S2 = S1 // 4
BLOCK = 64
TILES = 8


ORDER = (
    0, 1, 2, 3, 4, 5, 6, 14, 7, 9, 8, 11, 10, 17, 15, 12, 13, 46, 58, 47, 68, 43, 44, 48, 16, 18, 59, 55, 88, 45, 49,
    69, 52, 60, 61, 42, 50, 53, 54, 78, 71, 19, 70, 56, 90, 79, 51, 57, 91, 89, 62, 80, 81, 20, 72, 92, 82, 21, 22,
    63, 23, 73, 24, 26, 93, 83, 27, 28, 64, 74, 29, 30, 31, 94, 84, 32, 33, 75, 65, 66, 76, 34, 35, 36, 37, 85, 86,
    95, 96, 38, 39, 40, 41, 25, 67, 77, 87, 97,
)


def dot_nt(a, b, precision=None):
    return lax.dot_general(a, b, (((1,), (1,)), ((), ())), precision=precision, preferred_element_type=F32)


def dot_nn(a, b, precision=None):
    return lax.dot_general(a, b, (((1,), (0,)), ((), ())), precision=precision, preferred_element_type=F32)


def dot_tn(a, b, precision=None):
    return lax.dot_general(a, b, (((0,), (0,)), ((), ())), precision=precision, preferred_element_type=F32)


def split(v):
    high = v.astype(BF16)
    return high, (v - high.astype(F32)).astype(BF16)


def spread_row(v, r):
    return jnp.broadcast_to(v[r:r + 1, :], (8, 128))


def spread_lane(v, c):
    return jnp.broadcast_to(v[:, c:c + 1], (8, 128))


def eliminate(groups, g):
    sub = lax.broadcasted_iota(jnp.int32, (8, 128), 0)
    v = groups[g]
    c = [spread_lane(v, 8 * g + t) for t in range(8)]
    w, m = [None] * 8, {}
    for t in range(0, 8, 2):
        r0, r1 = spread_row(v, t), spread_row(v, t + 1)
        p, q, r = spread_row(c[t], t), spread_row(c[t + 1], t), spread_row(c[t + 1], t + 1)
        over = 1.0 / (p * r - q * q)
        po, qo, ro = p * over, q * over, r * over
        w[t], w[t + 1] = ro * r0 - qo * r1, po * r1 - qo * r0
        for u in range(t + 2, 8):
            pu, su = spread_row(c[u], t), spread_row(c[u], t + 1)
            m[t, u], m[t + 1, u] = ro * pu - qo * su, po * su - qo * pu
            c[u] = c[u] - (c[t] * m[t, u] + c[t + 1] * m[t + 1, u])
        new = v - (c[t] * w[t] + c[t + 1] * w[t + 1])
        v = jnp.where(sub > t + 1, new, jnp.where(sub == t + 1, r1 - (q / p) * r0, v))
    groups[g] = v
    if g + 1 == len(groups):
        return
    solved = list(w)
    for t in (4, 2, 0):
        for s in (t, t + 1):
            total = m[s, t + 2] * solved[t + 2]
            for u in range(t + 3, 8):
                total = total + m[s, u] * solved[u]
            solved[s] = w[s] - total
    for i in range(g + 1, len(groups)):
        p = [spread_lane(groups[i], 8 * g + t) * solved[t] for t in range(8)]
        groups[i] = groups[i] - (((p[0] + p[1]) + (p[2] + p[3])) + ((p[4] + p[5]) + (p[6] + p[7])))


N_PANEL = 13
N_GRAM = 19
N_CROSS = 4 * CHUNKS * 18


def body(
    panel_hbm, w_hbm,
    u_out, ih_out, il_out, w_ref, f_ref, bh_out, bl_out,
    panel_ref, wh_ref, wl_ref, a_ref, ab_ref, g1_ref, g2_ref, gz_ref, t_ref,
    c_ref, r1_ref, r2_ref, w_sem, send_sem, recv_sem,
):
    row = lax.axis_index("row")
    col = lax.axis_index("col")
    y, x = lax.div(row, 4), lax.rem(row, 4)
    z, k = lax.div(col, 2), lax.rem(col, 2)

    def step(v, d):
        return lax.rem(v + d, 4)

    def at_x(d):
        return (y * 4 + step(x, d), col)

    def at_y(d):
        return (step(y, d) * 4 + x, col)

    def piece(d, core):
        return step(z, d) * 2 + core

    def at_z(d):
        return (row, piece(d, k))

    partner = (row, z * 2 + 1 - k)

    def load_window(b):
        where = pl.ds(b * 256, 256)
        return pltpu.make_async_copy(w_hbm.at[where, :], w_ref.at[where, :], w_sem.at[b])

    load_panel = pltpu.make_async_copy(panel_hbm, panel_ref, w_sem.at[8])
    load_panel.start()
    for b in range(8):
        load_window(b).start()

    barrier = pltpu.get_barrier_semaphore()
    others = [at_x(d) for d in (1, 2, 3)] + [at_y(d) for d in (1, 2, 3)] + [at_z(d) for d in (1, 2, 3)] + [partner]
    for dev in others:
        pl.semaphore_signal(barrier, inc=1, device_id=dev, device_id_type=MESH)
    load_panel.wait()
    pl.semaphore_wait(barrier, len(others))

    sent = []

    def send(index, src, dst, dev):
        copy = pltpu.make_async_remote_copy(
            src_ref=src, dst_ref=dst, send_sem=send_sem.at[index], recv_sem=recv_sem.at[index],
            device_id=dev, device_id_type=MESH,
        )
        copy.start()
        sent.append(copy)
        return copy

    half = (pl.ds(0, 16), pl.ds(16, 16))
    up, down = at_z(1), at_z(3)
    own = {}
    own["up0"] = send(0, panel_ref.at[half[0]], a_ref.at[col, half[0]], up)
    own["down1"] = send(1, panel_ref.at[half[1]], a_ref.at[col, half[1]], down)
    own["up1"] = send(2, panel_ref.at[half[1]], a_ref.at[col, half[1]], up)
    own["down0"] = send(3, panel_ref.at[half[0]], a_ref.at[col, half[0]], down)
    own["partner"] = send(4, panel_ref, a_ref.at[col], partner)
    a_ref[col] = panel_ref[...]

    ops = []

    def split_window(b):
        rows = pl.ds(b * 256, 256)
        load_window(b).wait()
        high, low = split(w_ref[rows, :])
        wh_ref[rows, :] = high
        wl_ref[rows, :] = low

    for b in range(8):
        ops.append(lambda b=b: split_window(b))

    below, above, far = piece(3, k), piece(1, k), piece(2, k)
    gram_blocks = [None] * 4
    passed = {}

    def pass_on(index, who, h, dev):
        return send(index, a_ref.at[who, half[h]], a_ref.at[who, half[h]], dev)

    def pair_here(d, *needs):
        for copy in needs:
            copy.wait_recv()
        pair = a_ref[pl.ds(step(z, d) * 2, 2)].reshape(2 * PIECE, DEPTH)
        high, low = split(pair)
        ab_ref[d // 2, pl.ds(d % 2 * 64, 64), :] = high
        ab_ref[d // 2, pl.ds(HALF + d % 2 * 64, 64), :] = low
        gram_blocks[d] = dot_nt(panel_ref[...], pair, HIGHEST)

    @ops.append
    def _():
        own["down1"].wait_recv()
        passed["relay1"] = pass_on(6, above, 1, down)
        passed["above1"] = pass_on(8, above, 1, partner)

    @ops.append
    def _():
        own["up0"].wait_recv()
        passed["relay0"] = pass_on(5, below, 0, up)
        passed["below0"] = pass_on(7, below, 0, partner)

    @ops.append
    def _():
        own["down0"].wait_recv()
        passed["above0"] = pass_on(10, above, 0, partner)

    @ops.append
    def _():
        own["up1"].wait_recv()
        passed["below1"] = pass_on(9, below, 1, partner)

    @ops.append
    def _():
        passed["relay0"].wait_recv()
        passed["far0"] = pass_on(11, far, 0, partner)

    @ops.append
    def _():
        passed["relay1"].wait_recv()
        passed["far1"] = pass_on(12, far, 1, partner)

    ops.append(lambda: pair_here(0, own["partner"]))
    ops.append(lambda: pair_here(1, passed["above0"], passed["above1"]))
    ops.append(lambda: pair_here(2, passed["far0"], passed["far1"]))
    ops.append(lambda: pair_here(3, passed["below0"], passed["below1"]))

    gram = {}

    @ops.append
    def _():
        slab = pltpu.roll(jnp.concatenate(gram_blocks, axis=1), z * 2 * PIECE, 1)
        gram["first"] = []
        for part, (me, at) in enumerate(((x, at_x), (y, at_y))):
            g1_ref[part, me] = slab[part * 16:part * 16 + 16, :]
            gram["first"] += [
                send(N_PANEL + part * 3 + d - 1, g1_ref.at[part, me], g1_ref.at[part, me], at(d)) for d in (1, 2, 3)
            ]

    def summed(ref, part):
        return (ref[part, 0] + ref[part, 1]) + (ref[part, 2] + ref[part, 3])

    @ops.append
    def _():
        gram["second"] = []
        for part, (me, at) in enumerate(((y, at_y), (x, at_x))):
            for copy in gram["first"][part * 3:part * 3 + 3]:
                copy.wait_recv()
            g2_ref[part, me] = summed(g1_ref, part)
            gram["second"] += [
                send(N_PANEL + 6 + part * 3 + d - 1, g2_ref.at[part, me], g2_ref.at[part, me], at(d)) for d in (1, 2, 3)
            ]

    @ops.append
    def _():
        for part in range(2):
            for copy in gram["second"][part * 3:part * 3 + 3]:
                copy.wait_recv()
            gz_ref[col, part * 16:part * 16 + 16] = summed(g2_ref, part)
        gram["col"] = {d: send(N_PANEL + 12 + d - 1, gz_ref.at[col], gz_ref.at[col], at_z(d)) for d in (1, 3, 2)}
        gram["partner"] = [send(N_PANEL + 15, gz_ref.at[col], gz_ref.at[col], partner)]

    def gram_forward(d):
        gram["col"][d].wait_recv()
        there = gz_ref.at[piece(4 - d, k)]
        gram["partner"].append(send(N_PANEL + 15 + d, there, there, partner))

    for d in (1, 3, 2):
        ops.append(lambda d=d: gram_forward(d))

    @ops.append
    def _():
        for copy in gram["partner"]:
            copy.wait_recv()
        t_ref[:, :N] = gz_ref[...].reshape(N, N)
        rows_at = lax.broadcasted_iota(jnp.int32, (N, N), 0)
        cols_at = lax.broadcasted_iota(jnp.int32, (N, N), 1)
        t_ref[:, N:] = jnp.where(rows_at == cols_at, 1.0, 0.0).astype(F32)

    sub = lax.broadcasted_iota(jnp.int32, (BLOCK, 128), 0)
    lane = lax.broadcasted_iota(jnp.int32, (BLOCK, 128), 1)
    groups = []

    def tile_of(lo, at):
        e = t_ref[lo:lo + BLOCK, at // 128 * 128:at // 128 * 128 + 128]
        return pltpu.roll(e, 128 - at % 128, 1) if at % 128 else e

    def begin(e):
        e = jnp.where(lane < BLOCK, e, jnp.where(lane == sub + BLOCK, 1.0, 0.0).astype(F32))
        groups[:] = [e[8 * i:8 * i + 8, :] for i in range(BLOCK // 8)]

    def apply(b):
        lo, hi = b * BLOCK, b * BLOCK + BLOCK
        e = jnp.concatenate(groups, axis=0)
        diagonal = jnp.sum(jnp.where(lane == sub, e, 0.0), axis=1, keepdims=True)
        root = lax.rsqrt(diagonal)
        root = root * (1.5 - 0.5 * diagonal * root * root)
        inverse = (e * root)[:, BLOCK:2 * BLOCK]
        if hi < N:
            ahead = dot_nn(inverse, tile_of(lo, hi), HIGHEST)
            begin(tile_of(hi, hi) - dot_tn(ahead[:, :BLOCK], ahead, HIGHEST))
        done = dot_nn(inverse, t_ref[lo:lo + BLOCK, :], HIGHEST)
        t_ref[lo:lo + BLOCK, :] = done
        if hi < N:
            update = dot_tn(done[:, :N], done, HIGHEST)
            t_ref[hi:, :] -= update[hi:, :]

    @ops.append
    def _():
        rows_at = lax.broadcasted_iota(jnp.int32, (N, N), 0)
        cols_at = lax.broadcasted_iota(jnp.int32, (N, N), 1)
        u_out[...] = jnp.where(cols_at >= rows_at, t_ref[:, :N], 0.0)
        inverse = jnp.where(cols_at <= rows_at, t_ref[:, N:], 0.0)
        inverse = pltpu.roll(inverse, lax.rem(4 - z, 4) * 2 * PIECE, 1)
        ih, il = split(inverse)
        ih_out[...] = ih
        il_out[...] = il
        ah = jnp.concatenate([ab_ref[0, :HALF, :], ab_ref[1, :HALF, :]], axis=0)
        al = jnp.concatenate([ab_ref[0, HALF:, :], ab_ref[1, HALF:, :]], axis=0)
        qh, ql = split((dot_nn(ih, al) + dot_nn(il, ah)) + dot_nn(ih, ah))
        high, low = split((dot_tn(ih, ql) + dot_tn(il, qh)) + dot_tn(ih, qh))
        bh_out[...] = high
        bl_out[...] = low

    def pieces():
        begin(tile_of(0, 0))
        for b in range(N // BLOCK):
            for g in range(BLOCK // 8):
                eliminate(groups, g)
                if g in (1, 3, 5):
                    yield
                if g == 7:
                    apply(b)
                    yield

    work = pieces()
    for n in range(4 * N // BLOCK):
        ops.append(lambda: next(work))

    def rows_of(start, size, align):
        return pl.ds(pl.multiple_of(start, align), size)

    def product(h, d, part):
        where = rows_of(part * 1024 + step(y if part else x, d) * 256, 256, 256)
        both = dot_nt(wh_ref[where, :], ab_ref[h])
        low = dot_nt(wl_ref[where, :], ab_ref[h, :HALF, :])
        c_ref[h, where, :] = (both[:, HALF:] + low) + both[:, :HALF]

    for h in range(2):
        for d in range(4):
            for part in range(2):
                ops.append(lambda h=h, d=d, part=part: product(h, d, part))

    class Stream:
        def __init__(self, h, chunk, part):
            self.h = h
            self.at = (at_y, at_x) if part else (at_x, at_y)
            self.me = (y, x) if part else (x, y)
            self.start = part * 1024 + chunk * S1
            self.number = (h * CHUNKS + chunk) * 2 + part
            self.index = N_PANEL + N_GRAM + self.number * 18
            self.first, self.second, self.back, self.last = {}, {}, {}, {}

        def near(self, d, h):
            start = self.start + step(self.me[0], d) * 256
            return rows_of(start + h * (S1 // 2), S1 // 2, S1 // 2)

        def share(self, d):
            return rows_of(self.start + self.me[0] * 256 + step(self.me[1], d) * S2, S2, S2)

        def sum_out(self, slot, where, d):
            there = r1_ref.at[self.number, slot]
            self.first[slot] = send(self.index + slot, c_ref.at[self.h, where, :], there, self.at[0](d))

        def far_out(self):
            self.sum_out(0, self.near(2, 0), 1)
            self.sum_out(1, self.near(2, 1), 3)

        def near_out(self):
            self.sum_out(2, self.near(1, 1), 1)
            self.sum_out(3, self.near(3, 0), 3)

        def relay(self, slot):
            d = (1, 3)[slot]
            self.first[slot].wait_recv()
            where = self.near(d, slot)
            c_ref[self.h, where, :] += r1_ref[self.number, slot]
            self.sum_out(4 + slot, where, d)

        def turn(self):
            for slot in (2, 3, 4, 5):
                self.first[slot].wait_recv()
            for h, (a, b) in enumerate(((3, 4), (2, 5))):
                where = self.near(0, h)
                c_ref[self.h, where, :] += r1_ref[self.number, a] + r1_ref[self.number, b]
            for d in (2, 1, 3):
                there = r2_ref.at[self.number, d - 1]
                src = c_ref.at[self.h, self.share(d), :]
                self.second[d] = send(self.index + 5 + d, src, there, self.at[1](d))

        def complete(self):
            for d in (1, 2, 3):
                self.second[d].wait_recv()
            where = self.share(0)
            mine = c_ref[self.h, where, :] + r2_ref[self.number, 0]
            f_ref[self.h, where, :] = mine + (r2_ref[self.number, 1] + r2_ref[self.number, 2])
            there = f_ref.at[self.h, where, :]
            for d in (2, 1, 3):
                self.back[d] = send(self.index + 8 + d, there, there, self.at[1](d))

        def spread_out(self, slot, d, h, to):
            there = f_ref.at[self.h, self.near(d, h), :]
            self.last[slot] = send(self.index + 12 + slot, there, there, self.at[0](to))

        def spread(self):
            for d in (1, 2, 3):
                self.back[d].wait_recv()
            self.spread_out(0, 0, 0, 1)
            self.spread_out(1, 0, 1, 3)
            self.spread_out(2, 0, 1, 1)
            self.spread_out(3, 0, 0, 3)

        def hand_on(self, slot):
            self.last[slot].wait_recv()
            self.spread_out(4 + slot, (3, 1)[slot], slot, (1, 3)[slot])

        def end(self):
            for slot in (2, 3, 4, 5):
                self.last[slot].wait_recv()

    for h in range(2):
        for chunk in range(CHUNKS):
            for part in range(2):
                s = Stream(h, chunk, part)
                ops += [s.far_out, s.near_out, lambda s=s: s.relay(0), lambda s=s: s.relay(1), s.turn]
                ops += [s.complete, s.spread, lambda s=s: s.hand_on(0), lambda s=s: s.hand_on(1), s.end]

    assert sorted(ORDER) == list(range(len(ops)))
    for n in ORDER:
        ops[n]()
    for copy in sent:
        copy.wait_send()


def gather_and_factor(panel_cols, window_cols):
    vmem = pl.BlockSpec(memory_space=pltpu.VMEM)
    count = N_PANEL + N_GRAM + N_CROSS
    return pl.pallas_call(
        body,
        out_shape=(
            pltpu.VMEM((N, N), F32),
            pltpu.VMEM((N, N), BF16),
            pltpu.VMEM((N, N), BF16),
            pltpu.VMEM((SLAB, DEPTH), F32),
            pltpu.VMEM((2, SLAB, HALF), F32),
            pltpu.VMEM((N, DEPTH), BF16),
            pltpu.VMEM((N, DEPTH), BF16),
        ),
        in_specs=[pl.BlockSpec(memory_space=pltpu.HBM)] * 2,
        out_specs=(vmem,) * 7,
        scratch_shapes=[
            pltpu.VMEM((PIECE, DEPTH), F32),
            pltpu.VMEM((SLAB, DEPTH), BF16),
            pltpu.VMEM((SLAB, DEPTH), BF16),
            pltpu.VMEM((8, PIECE, DEPTH), F32),
            pltpu.VMEM((2, 2 * HALF, DEPTH), BF16),
            pltpu.VMEM((2, 4, 16, N), F32),
            pltpu.VMEM((2, 4, 16, N), F32),
            pltpu.VMEM((8, PIECE, N), F32),
            pltpu.VMEM((N, 2 * N), F32),
            pltpu.VMEM((2, SLAB, HALF), F32),
            pltpu.VMEM((4 * CHUNKS, 6, S1 // 2, HALF), F32),
            pltpu.VMEM((4 * CHUNKS, 3, S2, HALF), F32),
            pltpu.SemaphoreType.DMA((9,)),
            pltpu.SemaphoreType.DMA((count,)),
            pltpu.SemaphoreType.DMA((count,)),
        ],
        compiler_params=pltpu.CompilerParams(
            collective_id=0, has_side_effects=True, vmem_limit_bytes=54900000
        ),
        name="gather_and_factor",
    )(panel_cols, window_cols)


def subtract_body(u_ref, ih_ref, il_ref, w_ref, f_ref, bh_ref, bl_ref, u_out, top_out, out, r_ref, top_ref, sem):
    copies = [pltpu.make_async_copy(u_ref, u_out, sem.at[TILES])]
    copies[0].start()
    rows = SLAB // TILES
    for b in range(TILES):
        where = pl.ds(b * rows, rows)
        fh, fl = split(jnp.concatenate([f_ref[0, where, :], f_ref[1, where, :]], axis=1))
        bh = bh_ref[...]
        r_ref[where, :] = w_ref[where, :] - ((dot_nn(fh, bl_ref[...]) + dot_nn(fl, bh)) + dot_nn(fh, bh))
        copies.append(pltpu.make_async_copy(r_ref.at[where, :], out.at[where, :], sem.at[b]))
        copies[-1].start()
        if b == TILES - 2:
            mine = pl.ds(pl.multiple_of(lax.axis_index("row") * 128, 128), 128)
            fh, fl = split(jnp.concatenate([f_ref[0, mine, :], f_ref[1, mine, :]], axis=1))
            ih = ih_ref[...]
            top_ref[...] = (dot_nt(fh, il_ref[...]) + dot_nt(fl, ih)) + dot_nt(fh, ih)
            copies.append(pltpu.make_async_copy(top_ref, top_out, sem.at[TILES + 1]))
            copies[-1].start()
    for copy in copies:
        copy.wait()


def subtract(*given):
    vmem = pl.BlockSpec(memory_space=pltpu.VMEM)
    anywhere = pl.BlockSpec(memory_space=pl.ANY)
    return pl.pallas_call(
        subtract_body,
        out_shape=(
            jax.ShapeDtypeStruct((N, N), F32),
            jax.ShapeDtypeStruct((128, N), F32),
            jax.ShapeDtypeStruct((SLAB, DEPTH), F32),
        ),
        in_specs=[vmem] * 7,
        out_specs=(anywhere,) * 3,
        scratch_shapes=[
            pltpu.VMEM((SLAB, DEPTH), F32),
            pltpu.VMEM((128, N), F32),
            pltpu.SemaphoreType.DMA((TILES + 2,)),
        ],
        compiler_params=pltpu.CompilerParams(vmem_limit_bytes=24 * 2**20),
        name="subtract",
    )(*given)


def local(panel_cols, window_cols):
    return subtract(*gather_and_factor(panel_cols, window_cols))


def solution(mesh):
    return jax.shard_map(
        local,
        mesh=mesh,
        in_specs=(P("col", "row"), P("col", "row")),
        out_specs=(P(), P(("col", "row"), None), P("col", "row")),
        check_vma=False,
    )
```

time: 68.3 us -> 56.9 us (0.83)
  Pallas kernels: 66.5 us -> 55.9 us
  local copies, waits for them, and re-layouts: 0.9 us -> 0 us
    pallas_call x1, Pallas kernels: 61.2 us -> 51.3 us  [gather_and_factor(): pl.pallas_call(body, out_shape=(pltpu.VMEM((N, N), F32), pltpu.VMEM((N, N...]
    unnamed x2 -> x0, local copies, waits for them, and re-layouts: 0.9 us -> none
where the time goes in v4:
time: 56.9 us; the launch traced here: 56.7 us
  Pallas kernels  55.9 us (98%)
  between operations  0.8 us (1%)
    pallas_call x1, Pallas kernels, gather_and_factor(): pl.pallas_call(body, out_shape=(pltpu.VMEM((N, N), F32), pltpu.VMEM((N, N...  51.3 us
    pallas_call x1, Pallas kernels, subtract(): pl.pallas_call(subtract_body, out_shape=(jax.ShapeDtypeStruct((N, N), F32...  4.6 us

profile of v4, /device:TPU:0, one launch (start us, length us, event | category | flops | bytes accessed | tf_op | source)
XLA Modules:
  0.0 56.7 jit_solution(13780895527335066657)
XLA Ops:
  0.6 51.3 %gather_and_factor.1 = (f32[256,256]{1,0:T(8,128)S(1)}, bf16[256,256]{1,0:T(8,128)(2,1)S(1)}, bf16[256,256]{1,0:T(8,128)(2,1)S(1)}, f32[2048,1024]{1,0:T(8,128)S...) custom-call(f32[32,1024]{1,0:T(8,128)} %panel_hbm.1, ...), custom_call_target="tpu_custom_call" | custom-call | tf_op jit(solution)/shard_map/gather_and_factor/pallas_call | solution.py:445
  52.0 4.6 %subtract.1 = (f32[256,256]{1,0:T(8,128)}, f32[128,256]{1,0:T(8,128)}, f32[2048,1024]{1,0:T(8,128)}) custom-call(f32[256,256]{1,0:T(8,128)S(1)} %get-tuple-element.10.u_ref, bf16[256,256]{1,0:T(8,128)(2,1)S(1)} %get-tuple-element.11.ih_ref, bf16[256,256]{1,0:T(8,128)(2,1)S(1)} %get-tuple-element.12.il_ref, f32[2048,1024]{1,0:T(8,128)S(1)} %get-tuple-element.13.w_ref, ...), custom_call_target="tpu_custom_call" | custom-call | tf_op jit(solution)/shard_map/subtract/pallas_call | solution.py:507

commit v5 on v4

--- a/solution.py
+++ b/solution.py
@@ -23,10 +23,10 @@
 
 
 ORDER = (
-    0, 1, 2, 3, 4, 5, 6, 14, 7, 9, 8, 11, 10, 17, 15, 12, 13, 46, 58, 47, 68, 43, 44, 48, 16, 18, 59, 55, 88, 45, 49,
-    69, 52, 60, 61, 42, 50, 53, 54, 78, 71, 19, 70, 56, 90, 79, 51, 57, 91, 89, 62, 80, 81, 20, 72, 92, 82, 21, 22,
-    63, 23, 73, 24, 26, 93, 83, 27, 28, 64, 74, 29, 30, 31, 94, 84, 32, 33, 75, 65, 66, 76, 34, 35, 36, 37, 85, 86,
-    95, 96, 38, 39, 40, 41, 25, 67, 77, 87, 97,
+    0, 1, 2, 3, 4, 5, 6, 14, 7, 9, 8, 11, 10, 17, 15, 38, 50, 13, 12, 39, 60, 36, 40, 51, 37, 41, 61, 16, 18, 46, 70,
+    47, 80, 44, 52, 53, 63, 62, 48, 71, 49, 45, 34, 35, 42, 43, 19, 81, 72, 73, 82, 83, 54, 64, 20, 74, 84, 65, 55,
+    23, 21, 22, 75, 24, 85, 26, 56, 66, 27, 86, 76, 28, 29, 58, 67, 57, 68, 30, 77, 78, 87, 88, 31, 32, 33, 59, 69,
+    79, 89, 25,
 )
 
 
@@ -96,7 +96,7 @@
     panel_hbm, w_hbm,
     u_out, ih_out, il_out, w_ref, f_ref, bh_out, bl_out,
     panel_ref, wh_ref, wl_ref, a_ref, ab_ref, g1_ref, g2_ref, gz_ref, t_ref,
-    c_ref, r1_ref, r2_ref, w_sem, send_sem, recv_sem,
+    q_ref, c_ref, r1_ref, r2_ref, w_sem, send_sem, recv_sem,
 ):
     row = lax.axis_index("row")
     col = lax.axis_index("col")
@@ -231,7 +231,7 @@
         for part, (me, at) in enumerate(((x, at_x), (y, at_y))):
             g1_ref[part, me] = slab[part * 16:part * 16 + 16, :]
             gram["first"] += [
-                send(N_PANEL + part * 3 + d - 1, g1_ref.at[part, me], g1_ref.at[part, me], at(d)) for d in (1, 2, 3)
+                send(N_PANEL + part * 3 + d - 1, g1_ref.at[part, me], g1_ref.at[part, me], at(d)) for d in (2, 1, 3)
             ]
 
     def summed(ref, part):
@@ -245,7 +245,7 @@
                 copy.wait_recv()
             g2_ref[part, me] = summed(g1_ref, part)
             gram["second"] += [
-                send(N_PANEL + 6 + part * 3 + d - 1, g2_ref.at[part, me], g2_ref.at[part, me], at(d)) for d in (1, 2, 3)
+                send(N_PANEL + 6 + part * 3 + d - 1, g2_ref.at[part, me], g2_ref.at[part, me], at(d)) for d in (2, 1, 3)
             ]
 
     @ops.append
@@ -254,7 +254,7 @@
             for copy in gram["second"][part * 3:part * 3 + 3]:
                 copy.wait_recv()
             gz_ref[col, part * 16:part * 16 + 16] = summed(g2_ref, part)
-        gram["col"] = {d: send(N_PANEL + 12 + d - 1, gz_ref.at[col], gz_ref.at[col], at_z(d)) for d in (1, 3, 2)}
+        gram["col"] = {d: send(N_PANEL + 12 + d - 1, gz_ref.at[col], gz_ref.at[col], at_z(d)) for d in (2, 1, 3)}
         gram["partner"] = [send(N_PANEL + 15, gz_ref.at[col], gz_ref.at[col], partner)]
 
     def gram_forward(d):
@@ -298,6 +298,14 @@
             begin(tile_of(hi, hi) - dot_tn(ahead[:, :BLOCK], ahead, HIGHEST))
         done = dot_nn(inverse, t_ref[lo:lo + BLOCK, :], HIGHEST)
         t_ref[lo:lo + BLOCK, :] = done
+        xh, xl = split(pltpu.roll(done[:, N:], lax.rem(4 - z, 4) * 2 * PIECE, 1))
+        ih_out[lo:hi, :] = xh
+        il_out[lo:hi, :] = xl
+        ah = jnp.concatenate([ab_ref[0, :HALF, :], ab_ref[1, :HALF, :]], axis=0)
+        al = jnp.concatenate([ab_ref[0, HALF:, :], ab_ref[1, HALF:, :]], axis=0)
+        qh, ql = split((dot_nn(xh, al) + dot_nn(xl, ah)) + dot_nn(xh, ah))
+        q_ref[0, lo:hi, :] = qh
+        q_ref[1, lo:hi, :] = ql
         if hi < N:
             update = dot_tn(done[:, :N], done, HIGHEST)
             t_ref[hi:, :] -= update[hi:, :]
@@ -307,14 +315,7 @@
         rows_at = lax.broadcasted_iota(jnp.int32, (N, N), 0)
         cols_at = lax.broadcasted_iota(jnp.int32, (N, N), 1)
         u_out[...] = jnp.where(cols_at >= rows_at, t_ref[:, :N], 0.0)
-        inverse = jnp.where(cols_at <= rows_at, t_ref[:, N:], 0.0)
-        inverse = pltpu.roll(inverse, lax.rem(4 - z, 4) * 2 * PIECE, 1)
-        ih, il = split(inverse)
-        ih_out[...] = ih
-        il_out[...] = il
-        ah = jnp.concatenate([ab_ref[0, :HALF, :], ab_ref[1, :HALF, :]], axis=0)
-        al = jnp.concatenate([ab_ref[0, HALF:, :], ab_ref[1, HALF:, :]], axis=0)
-        qh, ql = split((dot_nn(ih, al) + dot_nn(il, ah)) + dot_nn(ih, ah))
+        ih, il, qh, ql = ih_out[...], il_out[...], q_ref[0], q_ref[1]
         high, low = split((dot_tn(ih, ql) + dot_tn(il, qh)) + dot_tn(ih, qh))
         bh_out[...] = high
         bl_out[...] = low
@@ -324,14 +325,13 @@
         for b in range(N // BLOCK):
             for g in range(BLOCK // 8):
                 eliminate(groups, g)
-                if g in (1, 3, 5):
+                if (b == 0 and g == 3) or (b > 0 and g in (1, 4)):
                     yield
-                if g == 7:
-                    apply(b)
-                    yield
+            apply(b)
+        yield
 
     work = pieces()
-    for n in range(4 * N // BLOCK):
+    for n in range(2 * N // BLOCK):
         ops.append(lambda: next(work))
 
     def rows_of(start, size, align):
@@ -465,6 +465,7 @@
             pltpu.VMEM((2, 4, 16, N), F32),
             pltpu.VMEM((8, PIECE, N), F32),
             pltpu.VMEM((N, 2 * N), F32),
+            pltpu.VMEM((2, N, DEPTH), BF16),
             pltpu.VMEM((2, SLAB, HALF), F32),
             pltpu.VMEM((4 * CHUNKS, 6, S1 // 2, HALF), F32),
             pltpu.VMEM((4 * CHUNKS, 3, S2, HALF), F32),

time: 56.9 us -> 56 us (0.984)
  Pallas kernels: 55.9 us -> 55.1 us
    pallas_call x1, Pallas kernels: 51.3 us -> 50.5 us  [gather_and_factor(): pl.pallas_call(body, out_shape=(pltpu.VMEM((N, N), F32), pltpu.VMEM((N, N...]
where the time goes in v5:
time: 56 us; the launch traced here: 55.9 us
  Pallas kernels  55.1 us (98%)
  between operations  0.8 us (1%)
    pallas_call x1, Pallas kernels, gather_and_factor(): pl.pallas_call(body, out_shape=(pltpu.VMEM((N, N), F32), pltpu.VMEM((N, N...  50.5 us
    pallas_call x1, Pallas kernels, subtract(): pl.pallas_call(subtract_body, out_shape=(jax.ShapeDtypeStruct((N, N), F32...  4.6 us

profile of v5, /device:TPU:0, one launch (start us, length us, event | category | flops | bytes accessed | tf_op | source)
XLA Modules:
  0.0 55.9 jit_solution(3487189058475804664)
XLA Ops:
  0.6 50.5 %gather_and_factor.1 = (f32[256,256]{1,0:T(8,128)S(1)}, bf16[256,256]{1,0:T(8,128)(2,1)S(1)}, bf16[256,256]{1,0:T(8,128)(2,1)S(1)}, f32[2048,1024]{1,0:T(8,128)S...) custom-call(f32[32,1024]{1,0:T(8,128)} %panel_hbm.1, ...), custom_call_target="tpu_custom_call" | custom-call | tf_op jit(solution)/shard_map/gather_and_factor/pallas_call | solution.py:445
  51.1 4.6 %subtract.1 = (f32[256,256]{1,0:T(8,128)}, f32[128,256]{1,0:T(8,128)}, f32[2048,1024]{1,0:T(8,128)}) custom-call(f32[256,256]{1,0:T(8,128)S(1)} %get-tuple-element.10.u_ref, bf16[256,256]{1,0:T(8,128)(2,1)S(1)} %get-tuple-element.11.ih_ref, bf16[256,256]{1,0:T(8,128)(2,1)S(1)} %get-tuple-element.12.il_ref, f32[2048,1024]{1,0:T(8,128)S(1)} %get-tuple-element.13.w_ref, ...), custom_call_target="tpu_custom_call" | custom-call | tf_op jit(solution)/shard_map/subtract/pallas_call | solution.py:508

commit v6 on v5

--- a/solution.py
+++ b/solution.py
@@ -23,10 +23,10 @@
 
 
 ORDER = (
-    0, 1, 2, 3, 4, 5, 6, 14, 7, 9, 8, 11, 10, 17, 15, 38, 50, 13, 12, 39, 60, 36, 40, 51, 37, 41, 61, 16, 18, 46, 70,
-    47, 80, 44, 52, 53, 63, 62, 48, 71, 49, 45, 34, 35, 42, 43, 19, 81, 72, 73, 82, 83, 54, 64, 20, 74, 84, 65, 55,
-    23, 21, 22, 75, 24, 85, 26, 56, 66, 27, 86, 76, 28, 29, 58, 67, 57, 68, 30, 77, 78, 87, 88, 31, 32, 33, 59, 69,
-    79, 89, 25,
+    0, 1, 2, 3, 4, 5, 14, 6, 7, 9, 8, 11, 10, 17, 15, 38, 50, 39, 60, 36, 12, 40, 51, 13, 41, 37, 61, 34, 35, 16, 18,
+    46, 70, 47, 80, 42, 43, 44, 52, 53, 62, 63, 49, 48, 71, 45, 81, 19, 72, 73, 82, 83, 54, 64, 20, 74, 84, 55, 65,
+    23, 22, 21, 75, 24, 85, 26, 56, 66, 27, 28, 76, 86, 29, 58, 67, 68, 57, 30, 31, 78, 77, 87, 88, 32, 33, 59, 25,
+    69, 79, 89,
 )
 
 

time: 56 us -> 54.2 us (0.968)
  Pallas kernels: 55.1 us -> 53.3 us
    pallas_call x1, Pallas kernels: 50.5 us -> 48.7 us  [gather_and_factor(): pl.pallas_call(body, out_shape=(pltpu.VMEM((N, N), F32), pltpu.VMEM((N, N...]
where the time goes in v6:
time: 54.2 us; the launch traced here: 54.1 us
  Pallas kernels  53.3 us (98%)
  between operations  0.8 us (1%)
    pallas_call x1, Pallas kernels, gather_and_factor(): pl.pallas_call(body, out_shape=(pltpu.VMEM((N, N), F32), pltpu.VMEM((N, N...  48.7 us
    pallas_call x1, Pallas kernels, subtract(): pl.pallas_call(subtract_body, out_shape=(jax.ShapeDtypeStruct((N, N), F32...  4.6 us

profile of v6, /device:TPU:0, one launch (start us, length us, event | category | flops | bytes accessed | tf_op | source)
XLA Modules:
  0.0 54.1 jit_solution(6198520448393882500)
XLA Ops:
  0.6 48.7 %gather_and_factor.1 = (f32[256,256]{1,0:T(8,128)S(1)}, bf16[256,256]{1,0:T(8,128)(2,1)S(1)}, bf16[256,256]{1,0:T(8,128)(2,1)S(1)}, f32[2048,1024]{1,0:T(8,128)S...) custom-call(f32[32,1024]{1,0:T(8,128)} %panel_hbm.1, ...), custom_call_target="tpu_custom_call" | custom-call | tf_op jit(solution)/shard_map/gather_and_factor/pallas_call | solution.py:445
  49.3 4.6 %subtract.1 = (f32[256,256]{1,0:T(8,128)}, f32[128,256]{1,0:T(8,128)}, f32[2048,1024]{1,0:T(8,128)}) custom-call(f32[256,256]{1,0:T(8,128)S(1)} %get-tuple-element.10.u_ref, bf16[256,256]{1,0:T(8,128)(2,1)S(1)} %get-tuple-element.11.ih_ref, bf16[256,256]{1,0:T(8,128)(2,1)S(1)} %get-tuple-element.12.il_ref, f32[2048,1024]{1,0:T(8,128)S(1)} %get-tuple-element.13.w_ref, ...), custom_call_target="tpu_custom_call" | custom-call | tf_op jit(solution)/shard_map/subtract/pallas_call | solution.py:508

commit v7 on v6

--- a/solution.py
+++ b/solution.py
@@ -23,10 +23,10 @@
 
 
 ORDER = (
-    0, 1, 2, 3, 4, 5, 14, 6, 7, 9, 8, 11, 10, 17, 15, 38, 50, 39, 60, 36, 12, 40, 51, 13, 41, 37, 61, 34, 35, 16, 18,
-    46, 70, 47, 80, 42, 43, 44, 52, 53, 62, 63, 49, 48, 71, 45, 81, 19, 72, 73, 82, 83, 54, 64, 20, 74, 84, 55, 65,
-    23, 22, 21, 75, 24, 85, 26, 56, 66, 27, 28, 76, 86, 29, 58, 67, 68, 57, 30, 31, 78, 77, 87, 88, 32, 33, 59, 25,
-    69, 79, 89,
+    0, 1, 2, 3, 4, 5, 6, 14, 7, 9, 8, 11, 10, 17, 15, 36, 39, 60, 37, 38, 50, 35, 12, 13, 40, 51, 41, 61, 34, 16, 18,
+    47, 80, 42, 46, 70, 49, 44, 45, 62, 63, 48, 52, 53, 71, 81, 43, 19, 82, 83, 73, 72, 64, 54, 20, 84, 74, 65, 55,
+    23, 21, 22, 85, 75, 24, 26, 66, 56, 27, 28, 86, 76, 29, 68, 58, 67, 57, 30, 31, 87, 88, 78, 77, 32, 33, 25, 69,
+    59, 89, 79,
 )
 
 

time: 54.2 us -> 56.1 us (1.035)
  Pallas kernels: 53.3 us -> 55.2 us
    pallas_call x1, Pallas kernels: 48.7 us -> 50.6 us  [gather_and_factor(): pl.pallas_call(body, out_shape=(pltpu.VMEM((N, N), F32), pltpu.VMEM((N, N...]
where the time goes in v7:
time: 56.1 us; the launch traced here: 56 us
  Pallas kernels  55.2 us (98%)
  between operations  0.8 us (1%)
    pallas_call x1, Pallas kernels, gather_and_factor(): pl.pallas_call(body, out_shape=(pltpu.VMEM((N, N), F32), pltpu.VMEM((N, N...  50.6 us
    pallas_call x1, Pallas kernels, subtract(): pl.pallas_call(subtract_body, out_shape=(jax.ShapeDtypeStruct((N, N), F32...  4.6 us

profile of v7, /device:TPU:0, one launch (start us, length us, event | category | flops | bytes accessed | tf_op | source)
XLA Modules:
  0.0 56.0 jit_solution(11166465930340074983)
XLA Ops:
  0.6 50.6 %gather_and_factor.1 = (f32[256,256]{1,0:T(8,128)S(1)}, bf16[256,256]{1,0:T(8,128)(2,1)S(1)}, bf16[256,256]{1,0:T(8,128)(2,1)S(1)}, f32[2048,1024]{1,0:T(8,128)S...) custom-call(f32[32,1024]{1,0:T(8,128)} %panel_hbm.1, ...), custom_call_target="tpu_custom_call" | custom-call | tf_op jit(solution)/shard_map/gather_and_factor/pallas_call | solution.py:445
  51.2 4.6 %subtract.1 = (f32[256,256]{1,0:T(8,128)}, f32[128,256]{1,0:T(8,128)}, f32[2048,1024]{1,0:T(8,128)}) custom-call(f32[256,256]{1,0:T(8,128)S(1)} %get-tuple-element.10.u_ref, bf16[256,256]{1,0:T(8,128)(2,1)S(1)} %get-tuple-element.11.ih_ref, bf16[256,256]{1,0:T(8,128)(2,1)S(1)} %get-tuple-element.12.il_ref, f32[2048,1024]{1,0:T(8,128)S(1)} %get-tuple-element.13.w_ref, ...), custom_call_target="tpu_custom_call" | custom-call | tf_op jit(solution)/shard_map/subtract/pallas_call | solution.py:508
